TPU v7x, 256 devices: a whole 4x4x8 slice. The times are simulated.
256 devices in a mesh: left: 16 (over z, y_hi), right: 16 (over y_lo, x, core).
Axes of the slice: x: 4, y: 4 (y_hi: 2, y_lo: 2; y = y_hi * 2 + y_lo), z: 8, core: 2. Of those that a mesh axis runs over, the one named last changes fastest.
Arguments:
- left_table: float32 [32768, 400], P(('left', 'right')), may hold values from -2 to 2
- left_state: float32 [32768], P(('left', 'right')), may hold values from 0.05 to 0.5
- right_table: float32 [32768, 400], P(('left', 'right')), may hold values from -2 to 2
- right_state: float32 [32768], P(('left', 'right')), may hold values from 0.05 to 0.5
- relation_table: float32 [256, 400], replicated, may hold values from -6 to 6
- relation_state: float32 [256], replicated, may hold values from 0.05 to 0.5
- source_ids: int32 [16, 16, 1024], P('left', 'right'), may hold values from 0 to 2047
- target_ids: int32 [16, 16, 1024], P('left', 'right'), may hold values from 0 to 2047
- relation_ids: int32 [16, 16, 1024], P('left', 'right'), may hold values from 0 to 255
- negative_ids: int32 [16, 16, 2, 1024], P('left', 'right'), may hold values from 0 to 2047
Outputs:
- left_new: float32 [32768, 400], P(('left', 'right'))
- left_state_new: float32 [32768], P(('left', 'right'))
- right_new: float32 [32768, 400], P(('left', 'right'))
- right_state_new: float32 [32768], P(('left', 'right'))
- relation_new: float32 [256, 400], replicated
- relation_state_new: float32 [256], replicated
All inputs are finite; a program needn't handle non-finite values.
Results may differ from a plain program's by a relative error of at most 0.0021.
Values may be sent and summed in bfloat16 or wider, within the bound.
A program may use at most 64 MiB of HBM per device.

v0:
```python
import jax
import jax.numpy as jnp
from jax import lax
from jax.sharding import PartitionSpec as P

LEARN_RATE = 0.1
NEG_WEIGHT = 0.03125


def from_behind(value, axis, by):
    devices = lax.axis_size(axis)
    return lax.ppermute(value, axis, [(i, (i + by) % devices) for i in range(devices)])


def complex_product(first, second):
    half_width = first.shape[-1] // 2
    a_re, a_im = (first[..., :half_width], first[..., half_width:])
    b_re, b_im = (second[..., :half_width], second[..., half_width:])
    return jnp.concatenate([a_re * b_re - a_im * b_im, a_re * b_im + a_im * b_re], axis=-1)


def complex_back(grad, other):
    half_width = grad.shape[-1] // 2
    g_re, g_im = (grad[..., :half_width], grad[..., half_width:])
    o_re, o_im = (other[..., :half_width], other[..., half_width:])
    return jnp.concatenate([g_re * o_re + g_im * o_im, g_im * o_re - g_re * o_im], axis=-1)


def adagrad(table, state, grad):
    state_new = state + jnp.mean(grad * grad, axis=-1)
    return (table - LEARN_RATE * grad / jnp.sqrt(state_new)[:, None], state_new)


def one_hot_rows(ids, count):
    columns = jnp.arange(count, dtype=jnp.int32)
    return (ids[:, None] == columns[None, :]).astype(jnp.bfloat16)


def per_device(
    left_table,
    left_state,
    right_table,
    right_state,
    relation_table,
    relation_state,
    source_ids,
    target_ids,
    relation_ids,
    negative_ids,
):
    row_count = left_table.shape[0]
    width = left_table.shape[1]
    source = source_ids.reshape(-1)
    target = target_ids.reshape(-1)
    relation = relation_ids.reshape(-1)
    negative = negative_ids.reshape(negative_ids.shape[2], negative_ids.shape[3])
    groups = negative.shape[0]
    edge_count = source.shape[0]
    moved_table, moved_state = from_behind((right_table, right_state), "right", 1)
    right_part = lax.all_gather(moved_table.astype(jnp.bfloat16), "left", axis=0, tiled=True)
    piece = lax.all_gather(left_table.astype(jnp.bfloat16), "right", axis=0, tiled=True)
    onehot = one_hot_rows(source, piece.shape[0])
    source_emb = jnp.dot(onehot, piece, preferred_element_type=jnp.float32)
    target_hot = one_hot_rows(target, right_part.shape[0])
    target_embedding = jnp.dot(target_hot, right_part, preferred_element_type=jnp.float32)
    relation_bf = relation_table.astype(jnp.bfloat16)
    relation_hot = one_hot_rows(relation, relation_table.shape[0])
    relation_emb = jnp.dot(relation_hot, relation_bf, preferred_element_type=jnp.float32)
    query = complex_product(source_emb, relation_emb)
    positive = jnp.sum(query * target_embedding, axis=-1)
    query_block_rows = query.astype(jnp.bfloat16).reshape(groups, -1, width)
    negative_rows = jnp.take(right_part, negative, axis=0)
    score_matrix = jnp.einsum(
        "wet,wjt->wej", query_block_rows, negative_rows, preferred_element_type=jnp.float32
    )
    positive_score_grad = -jax.nn.sigmoid(-positive)
    negative_score_grad = (NEG_WEIGHT * jax.nn.sigmoid(score_matrix)).astype(jnp.bfloat16)
    from_negatives = jnp.einsum(
        "fjs,fsh->fjh", negative_score_grad, negative_rows, preferred_element_type=jnp.float32
    )
    query_gradient = positive_score_grad[:, None] * target_embedding + from_negatives.reshape(
        edge_count, width
    )
    negative_embedding_grad = (
        jnp.einsum(
            "fre,frl->fel",
            negative_score_grad,
            query_block_rows,
            preferred_element_type=jnp.float32,
        )
        .astype(jnp.bfloat16)
        .reshape(-1, width)
    )
    target_grad = (positive_score_grad[:, None] * query).astype(jnp.bfloat16)
    source_grad = complex_back(query_gradient, relation_emb).astype(jnp.bfloat16)
    relation_grad = complex_back(query_gradient, source_emb).astype(jnp.bfloat16)
    relation_term = jnp.einsum(
        "er,ed->rd", relation_hot, relation_grad, preferred_element_type=jnp.float32
    )
    onehot = one_hot_rows(source, lax.axis_size("right") * row_count)
    left_grad = lax.psum_scatter(
        jnp.einsum("er,ed->rd", onehot, source_grad, preferred_element_type=jnp.float32),
        "right",
        scatter_dimension=0,
        tiled=True,
    )
    all_ids = jnp.concatenate([target, negative.reshape(-1)])
    all_grads = jnp.concatenate([target_grad, negative_embedding_grad], axis=0)
    onehot = one_hot_rows(all_ids, lax.axis_size("left") * row_count)
    right_grad = lax.psum_scatter(
        jnp.einsum("er,ed->rd", onehot, all_grads, preferred_element_type=jnp.float32),
        "left",
        scatter_dimension=0,
        tiled=True,
    )
    left_new, left_state_new = adagrad(left_table, left_state, left_grad)
    right_new, right_state_new = adagrad(moved_table, moved_state, right_grad)
    relation_total = lax.psum(relation_term, ("left", "right"))
    relation_new, relation_state_new = adagrad(relation_table, relation_state, relation_total)
    return (left_new, left_state_new, right_new, right_state_new, relation_new, relation_state_new)


def solution(mesh):
    return jax.shard_map(
        per_device,
        mesh=mesh,
        in_specs=(
            P(("left", "right"), None),
            P(("left", "right")),
            P(("left", "right"), None),
            P(("left", "right")),
            P(),
            P(),
            P("left", "right", None),
            P("left", "right", None),
            P("left", "right", None),
            P("left", "right", None, None),
        ),
        out_specs=(
            P(("left", "right"), None),
            P(("left", "right")),
            P(("left", "right"), None),
            P(("left", "right")),
            P(),
            P(),
        ),
        check_vma=False,
    )
```

profile of v0, /device:TPU:1, one launch (start us, length us, event | category | flops | bytes accessed | tf_op | source)
XLA Modules:
  0.0 657.7 jit_solution(7649774851200412998)
XLA Ops:
  7.2 1.6 convert_element_type.13
  8.9 2.7 collective-permute-start
  11.5 3.0 collective-permute-done
  16.7 1.5 fusion.13
  18.3 34.3 %all-gather.3.cloned.1.call-done = bf16[2048,400]{0,1:T(8,128)(2,1)} async-done(((bf16[128,400]{0,1:T(8,128)(2,1)}), bf16[2048,400]{0,1:T(8,128)(2,1)}) %all-gather.3.cloned.1.call-update) | async-done | bytes 1638416 | tf_op jit(solution)/shard_map/all_gather | solution.py:61
  52.5 3.5 fusion.3
  56.1 1.5 fusion.34
  58.6 73.0 %all-gather.5.cloned.1.call-done = bf16[2048,400]{0,1:T(8,128)(2,1)} async-done(((bf16[128,400]{0,1:T(8,128)(2,1)}), bf16[2048,400]{0,1:T(8,128)(2,1)}) %all-gather.5.cloned.1.call-update) | async-done | bytes 1638416 | tf_op jit(solution)/shard_map/all_gather | solution.py:60
  131.7 2.8 copy.24
  134.4 9.2 %gather_fusion = bf16[2048,400]{1,0:T(8,128)(2,1)} fusion(bf16[2048,400]{1,0:T(8,128)(2,1)S(1)} %copy.24, s32[2048]{0:T(1024)S(1)} %bitcast_clamp_fusion), kind=kCustom, calls=%fused_computation | custom fusion | bytes 3284992 | tf_op jit(solution)/shard_map/jit(_take)/gather | solution.py:72
  143.6 4.1 copy.25
  147.7 2.2 multiply_reduce_fusion
  149.9 1.8 multiply_convert_fusion
  155.9 1.3 fusion.12
  157.4 3.9 fusion.2
  162.5 2.6 fusion.11
  165.2 7.8 %fusion = f32[2048,400]{0,1:T(8,128)} fusion(s32[3072]{0:T(1024)S(1)} %pad_add_fusion, bf16[2048,400]{0,1:T(8,128)(2,1)S(1)} %bitcast.39, bf16[1024,400]{0,1:T(8,128)(2,1)S(1)} %get-tuple-element.24), kind=kOutput, calls=%fused_computation.2 | convolution fusion | flops 5044371456 | bytes 5746688 | tf_op jit(solution)/shard_map/er,ed->rd/dot_general | solution.py:111
  173.7 5.9 collective-permute-start.1
  179.6 229.6 %all-reduce.2.cloned.1.call-done = f32[256,400]{0,1:T(8,128)} async-done(((f32[256,400]{0,1:T(8,128)}), f32[256,400]{0,1:T(8,128)}) %all-reduce.2.cloned.1.call-update) | async-done | bytes 409616 | tf_op jit(solution)/shard_map/psum | solution.py:118
  410.8 1.8 divide_subtract_fusion
  412.6 62.8 %reduce-scatter.3.cloned.1.call-done = f32[128,400]{0,1:T(8,128)} async-done(((f32[2048,400]{0,1:T(8,128)}), f32[128,400]{0,1:T(8,128)}) %reduce-scatter.3.cloned.1.call-update) | async-done | bytes 204816 | tf_op jit(solution)/shard_map/reduce_scatter | solution.py:101
  476.9 169.5 %reduce-scatter.5.cloned.1.call-done = f32[128,400]{0,1:T(8,128)} async-done(((f32[2048,400]{0,1:T(8,128)}), f32[128,400]{0,1:T(8,128)}) %reduce-scatter.5.cloned.1.call-update) | async-done | bytes 204816 | tf_op jit(solution)/shard_map/reduce_scatter | solution.py:110
  647.9 1.6 divide_subtract_fusion.1
  649.5 1.6 divide_subtract_fusion.2
  (71 shorter events, 14.2 us)
Async XLA Ops:
  7.2 45.4 %copy-start.17 = (s32[1,1,1024]{2,1,0:T(1,128)S(1)}, s32[1,1,1024]{2,1,0:T(1,128)}, u32[]{:S(2)}) copy-start(s32[1,1,1024]{2,1,0:T(1,128)} %param.16) | copy-start | bytes 12292
  7.2 45.4 %all-gather.3.cloned.1.call-start = ((), (), s32[]{:S(2)}) async-start(), calls=%async_computation.2 | async-start | bytes 1740800 | tf_op jit(solution)/shard_map/all_gather | solution.py:61
  8.8 122.8 %all-gather.5.cloned.1.call-start = ((), (), s32[]{:S(2)}) async-start(), calls=%async_computation.3 | async-start | bytes 1740800 | tf_op jit(solution)/shard_map/all_gather | solution.py:60
  8.9 5.7 collective-permute-start
  15.2 393.9 %all-reduce.2.cloned.1.call-start = ((), (), s32[]{:S(2)}) async-start(), calls=%async_computation.6 | async-start | bytes 819200 | tf_op jit(solution)/shard_map/psum | solution.py:118
  18.2 37.8 %copy-start = (f32[1024,400]{0,1:T(8,128)}, f32[1024,400]{0,1:T(8,128)S(1)}, u32[]{:S(2)}) copy-start(f32[1024,400]{0,1:T(8,128)S(1)} %fusion.13) | copy-start | bytes 4915204
  56.1 1.5 copy-start.2
  57.7 1.0 copy-start.9
  143.6 4.1 copy-start.4
  143.6 4.1 copy-start.5
  143.6 4.1 copy-start.14
  147.7 2.2 copy-start.6
  147.7 2.2 copy-start.10
  151.7 1.3 copy-start.19
  153.3 1.4 copy-start.1
  153.3 1.9 copy-start.3
  157.2 318.2 %reduce-scatter.3.cloned.1.call-start = ((), (), s32[]{:S(2)}) async-start(), calls=%async_computation.4 | async-start | bytes 3481600 | tf_op jit(solution)/shard_map/reduce_scatter | solution.py:101
  161.3 1.2 copy-start.11
  161.3 485.0 %reduce-scatter.5.cloned.1.call-start = ((), (), s32[]{:S(2)}) async-start(), calls=%async_computation.5 | async-start | bytes 3481600 | tf_op jit(solution)/shard_map/reduce_scatter | solution.py:110
  173.1 237.1 %copy-start.15 = (f32[256]{0:T(256)S(1)}, f32[256]{0:T(256)}, u32[]{:S(2)}) copy-start(f32[256]{0:T(256)} %param.15) | copy-start | bytes 3076
  173.1 237.7 %copy-start.7 = (f32[256,400]{0,1:T(8,128)S(1)}, f32[256,400]{0,1:T(8,128)}, u32[]{:S(2)}) copy-start(f32[256,400]{0,1:T(8,128)} %param.14) | copy-start | bytes 1228804
  173.7 302.7 %copy-start.16 = (f32[128]{0:T(128)S(1)}, f32[128]{0:T(128)}, u32[]{:S(2)}) copy-start(f32[128]{0:T(128)} %param.11) | copy-start | bytes 1540
  173.7 475.8 %copy-start.8 = (f32[128,400]{0,1:T(8,128)S(1)}, f32[128,400]{0,1:T(8,128)}, u32[]{:S(2)}) copy-start(f32[128,400]{0,1:T(8,128)} %param.10) | copy-start | bytes 614404
  173.7 473.6 %collective-permute-start.1 = (f32[128]{0:T(128)S(1)}, f32[128]{0:T(128)S(1)}, u32[]{:S(2)}, u32[]{:S(2)}) collective-permute-start(f32[128]{0:T(128)S(1)} %copy-done.18), channel_id=1, source_target_pairs={{0,1},{1,2},{2,3},{3,4},{4,5},{5,6},{6,7},{7,8},{8,9},{9,10},{10,1... | collective-permute-start | bytes 1544 | tf_op jit(solution)/shard_map/ppermute | solution.py:12
  (3 other events, 2.0 us)
Sparse Core Ops, SparseCore 0:
  10.3 42.1 all-gather.2
  55.6 76.0 all-gather.4
  157.3 251.8 all-reduce.1
  411.6 63.7 reduce-scatter.2
  479.2 167.0 reduce-scatter.4
where the time goes:
time: 662 us; the launch traced here: 658 us
  waiting for transfers between devices  572 us (86%)
  matrix products  25.7 us (4%)
  local copies, waits for them, and re-layouts  20.5 us (3%)
  other arithmetic  16.3 us (2%)
  between operations  14 us (2%)
  starting transfers between devices  8.91 us (1%)
    psum x1, waiting for transfers between devices, per_device(): relation_total = lax.psum(relation_term, ('left', 'right'))  230 us
    reduce_scatter x1, waiting for transfers between devices, per_device(): lax.psum_scatter(jnp.einsum('er,ed->rd', onehot, all_grads, preferred_ele...  169 us
    all_gather x1, waiting for transfers between devices, per_device(): lax.all_gather(moved_table.astype(jnp.bfloat16), 'left', axis=0, tiled=True)  73 us
    reduce_scatter x1, waiting for transfers between devices, per_device(): lax.psum_scatter(jnp.einsum('er,ed->rd', onehot, source_grad, preferred_e...  62.8 us
    all_gather x1, waiting for transfers between devices, per_device(): lax.all_gather(left_table.astype(jnp.bfloat16), 'right', axis=0, tiled=True)  34.3 us
    gather x2, local copies, waits for them, and re-layouts, per_device(): negative_rows = jnp.take(right_part, negative, axis=0)  13.2 us
  transfers between devices with their start and end apart: 7, of which 6 were waited for; matrix products, arithmetic and copies ran while one was open for 4% of the time, Pallas kernels for 0%

commit v1 on v0

v1 whole, which is shorter than its diff:
```python
import functools

import jax
import jax.numpy as jnp
from jax import lax
from jax.experimental import pallas as pl
from jax.experimental.pallas import tpu as pltpu
from jax.sharding import PartitionSpec as P

LEARN_RATE = 0.1
NEG_WEIGHT = 0.03125
MESH = pl.DeviceIdType.MESH
F32, BF16 = jnp.float32, jnp.bfloat16

N = 16
W = 400
HALF = 200
B = 128
LOW = 208
HIGH = W - LOW
VMEM_LIMIT = 60 * 1024 * 1024


def mod(value, n):
    return lax.rem(value + 4 * n, n)


class Place:
    def __init__(self):
        self.l = lax.axis_index("left")
        self.r = lax.axis_index("right")
        self.z = lax.div(self.l, 2)
        self.h = lax.rem(self.l, 2)
        self.c = lax.rem(self.r, 2)
        self.x = lax.rem(lax.div(self.r, 2), 4)
        self.yl = lax.div(self.r, 8)

    def left_at(self, z, k=0):
        h = self.h if k == 0 else 1 - self.h
        return mod(self.z + z, 8) * 2 + h

    def right_at(self, x, k=0, other=0):
        yl = self.yl if k == 0 else 1 - self.yl
        c = self.c if other == 0 else 1 - self.c
        return (yl * 4 + mod(self.x + x, 4)) * 2 + c


def remote(src, dst, send, recv, left, right):
    return pltpu.make_async_remote_copy(
        src_ref=src,
        dst_ref=dst,
        send_sem=send,
        recv_sem=recv,
        device_id=(left, right),
        device_id_type=MESH,
    )


def greet(peers):
    barrier = pltpu.get_barrier_semaphore()
    for left, right in peers:
        pl.semaphore_signal(barrier, inc=1, device_id=(left, right), device_id_type=MESH)
    pl.semaphore_wait(barrier, len(peers))


def gather_kernel(lt, rt, table, state, lg, rg, moved, moved_state, ss, rs, ls, lr, ms):
    me = Place()
    l, r = me.l, me.r
    ahead, behind = mod(r + 1, N), mod(r - 1, N)
    l_other = me.left_at(0, 1)
    zp, zm = me.left_at(1), me.left_at(-1)
    xp, xm = me.right_at(1), me.right_at(-1)
    yo, co = me.right_at(0, 1), me.right_at(0, 0, 1)
    barrier = pltpu.get_barrier_semaphore()
    to = [(l, ahead), (l_other, ahead), (l, behind), (l_other, behind), (zp, r), (zm, r)]
    to += [(l, xp), (l, xm), (l, yo), (l, co)]
    for a, b in to:
        pl.semaphore_signal(barrier, inc=1, device_id=(a, b), device_id_type=MESH)
    own = pltpu.make_async_copy(lt, lg.at[r], ms.at[4])
    own.start()
    pl.semaphore_wait(barrier, len(to))

    sends = []

    def send(src, dst, s, d, left, right):
        copy = remote(src, dst, s, d, left, right)
        copy.start()
        sends.append(copy)

    def arrived(dst, d):
        remote(dst, dst, ms.at[5], d, l, co).wait_recv()

    send(rt, rg.at[l], ss.at[0], rs.at[0], l, ahead)
    send(rt, rg.at[l], ss.at[1], rs.at[1], l_other, ahead)
    send(lt, lg.at[r], ls.at[0], lr.at[0], l, yo)
    send(lt, lg.at[r], ls.at[1], lr.at[1], l, xp)
    send(lt, lg.at[r], ls.at[2], lr.at[2], l, xm)
    send(lt, lg.at[r], ls.at[3], lr.at[3], l, co)

    lslot = lambda x, k=0: me.right_at(x, k)
    slot = lambda z, k: me.left_at(z, k)

    arrived(rg.at[l], rs.at[0])
    send(rg.at[l], rg.at[l], ss.at[2], rs.at[2], zp, r)
    send(rg.at[l], rg.at[l], ss.at[3], rs.at[3], zm, r)
    arrived(lg.at[yo], lr.at[0])
    send(lg.at[yo], lg.at[yo], ls.at[4], lr.at[4], l, xp)
    send(lg.at[yo], lg.at[yo], ls.at[5], lr.at[5], l, xm)
    send(lg.at[yo], lg.at[yo], ls.at[6], lr.at[6], l, co)
    arrived(rg.at[l_other], rs.at[1])
    send(rg.at[l_other], rg.at[l_other], ss.at[4], rs.at[4], zp, r)
    send(rg.at[l_other], rg.at[l_other], ss.at[5], rs.at[5], zm, r)
    send(table, moved, ms.at[0], ms.at[1], l, ahead)
    send(state, moved_state, ms.at[2], ms.at[3], l, ahead)

    def ring(d, k):
        i = 2 + 4 * (d - 1) + 2 * k
        a, b = slot(-d, k), slot(d, k)
        n = 6 + 4 * (d - 1) + 2 * k
        if d < 3:
            arrived(rg.at[a], rs.at[i])
            send(rg.at[a], rg.at[a], ss.at[n], rs.at[n], zp, r)
            arrived(rg.at[b], rs.at[i + 1])
            send(rg.at[b], rg.at[b], ss.at[n + 1], rs.at[n + 1], zm, r)
        else:
            low, high = pl.ds(0, LOW), pl.ds(LOW, HIGH)
            arrived(rg.at[a], rs.at[i])
            send(rg.at[a, low], rg.at[a, low], ss.at[n], rs.at[n], zp, r)
            arrived(rg.at[b], rs.at[i + 1])
            send(rg.at[b, high], rg.at[b, high], ss.at[n + 1], rs.at[n + 1], zm, r)

    def across(k):
        a, b = lslot(-1, k), lslot(1, k)
        ra, rb = (1, 2) if k == 0 else (4, 5)
        i = 7 + 4 * k
        low, high = pl.ds(0, LOW), pl.ds(LOW, HIGH)
        arrived(lg.at[a], lr.at[ra])
        send(lg.at[a, low], lg.at[a, low], ls.at[i], lr.at[i], l, xp)
        send(lg.at[a], lg.at[a], ls.at[i + 2], lr.at[i + 2], l, co)
        arrived(lg.at[b], lr.at[rb])
        send(lg.at[b, high], lg.at[b, high], ls.at[i + 1], lr.at[i + 1], l, xm)
        send(lg.at[b], lg.at[b], ls.at[i + 3], lr.at[i + 3], l, co)

    def far(k):
        a = lslot(2, k)
        i = 7 + 4 * k
        arrived(lg.at[a, pl.ds(0, LOW)], lr.at[i])
        arrived(lg.at[a, pl.ds(LOW, HIGH)], lr.at[i + 1])
        send(lg.at[a], lg.at[a], ls.at[15 + k], lr.at[15 + k], l, co)

    across(0)
    ring(1, 0)
    across(1)
    ring(1, 1)
    ring(2, 0)
    far(0)
    ring(2, 1)
    far(1)
    ring(3, 0)
    ring(3, 1)
    for x, k, i in ((0, 0, 3), (0, 1, 6), (-1, 0, 9), (1, 0, 10), (-1, 1, 13), (1, 1, 14), (2, 0, 15), (2, 1, 16)):
        arrived(lg.at[me.right_at(x, k, 1)], lr.at[i])
    for k in (0, 1):
        a = slot(4, k)
        arrived(rg.at[a, pl.ds(0, LOW)], rs.at[14 + 2 * k])
        arrived(rg.at[a, pl.ds(LOW, HIGH)], rs.at[15 + 2 * k])
    arrived(moved, ms.at[1])
    arrived(moved_state, ms.at[3])
    own.wait()
    for copy in sends:
        copy.wait_send()


def gather(lt, rt, table, state):
    vm = pl.BlockSpec(memory_space=pltpu.VMEM)
    return pl.pallas_call(
        gather_kernel,
        out_shape=(
            jax.ShapeDtypeStruct((N, W, B), BF16),
            jax.ShapeDtypeStruct((N, W, B), BF16),
            jax.ShapeDtypeStruct((B, W), F32),
            jax.ShapeDtypeStruct((1, B), F32),
        ),
        in_specs=[vm] * 4,
        out_specs=(vm,) * 4,
        scratch_shapes=[
            pltpu.SemaphoreType.DMA((18,)),
            pltpu.SemaphoreType.DMA((18,)),
            pltpu.SemaphoreType.DMA((17,)),
            pltpu.SemaphoreType.DMA((17,)),
            pltpu.SemaphoreType.DMA((6,)),
        ],
        compiler_params=pltpu.CompilerParams(collective_id=0, has_side_effects=True, vmem_limit_bytes=VMEM_LIMIT),
        name="gather_parts",
    )(lt, rt, table, state)


T = 256
STEPS = 4
J = 256
JS = 8


def one_hot(ids, first, rows):
    row = lax.broadcasted_iota(jnp.int32, (rows, ids.shape[-1]), 0) + first
    return row == ids


def back(g, o):
    g_re, g_im, o_re, o_im = g[:HALF], g[HALF:], o[:HALF], o[HALF:]
    return jnp.concatenate([g_re * o_re + g_im * o_im, g_im * o_re - g_re * o_im], axis=0)


def dot(a, b):
    return lax.dot_general(a, b, (((1,), (0,)), ((), ())), preferred_element_type=F32)


def dot_nt(a, b):
    return lax.dot_general(a, b, (((1,), (1,)), ((), ())), preferred_element_type=F32)


def bucket_kernel(lg, rg, rel, src, rid, tgt, neg, lout, rout, pout, rn, ohs, ohr, w, qs, sg, og, mult):
    for i in range(N):
        rn[pl.ds(i * B, B), :] = rg[i].T
    for j in range(JS):
        for c in range(2):
            hit = jnp.where(one_hot(neg[c], j * J, J), 1.0, 0.0)
            count = jnp.sum(hit, axis=1, keepdims=True) * NEG_WEIGHT
            mult[c, pl.ds(j * J, J), :] = jnp.broadcast_to(count, (J, B))
    lcat = lambda: jnp.concatenate([lg[i] for i in range(N)], axis=1)
    rcat = lambda: jnp.concatenate([rg[i] for i in range(N)], axis=1)

    def step(t, _):
        c = lax.div(t, 2)
        for j in range(JS):
            ohs[t, pl.ds(j * J, J), :] = jnp.where(one_hot(src[t], j * J, J), 1.0, 0.0).astype(BF16)
        ohr[t] = jnp.where(one_hot(rid[t], 0, 256), 1.0, 0.0).astype(BF16)
        s = dot(lcat(), ohs[t])
        o = dot(rel[...], ohr[t])
        s_re, s_im, o_re, o_im = s[:HALF], s[HALF:], o[:HALF], o[HALF:]
        q = jnp.concatenate([s_re * o_re - s_im * o_im, s_re * o_im + s_im * o_re], axis=0).astype(BF16)
        qs[t] = q
        positive = jnp.zeros((1, T), F32)
        for j in range(JS):
            score = dot(rn[pl.ds(j * J, J), :], q)
            hit = one_hot(tgt[t], j * J, J)
            positive += jnp.sum(jnp.where(hit, score, 0.0), axis=0, keepdims=True)
            m = mult[c, pl.ds(j * J, J), :]
            m = jnp.concatenate([m, m], axis=1)
            w[t, pl.ds(j * J, J), :] = (jax.nn.sigmoid(score) * m).astype(BF16)
        pos_grad = -jax.nn.sigmoid(-positive)
        for j in range(JS):
            hit = one_hot(tgt[t], j * J, J)
            old = w[t, pl.ds(j * J, J), :].astype(F32)
            w[t, pl.ds(j * J, J), :] = (old + jnp.where(hit, pos_grad, 0.0)).astype(BF16)
        g = dot(rcat(), w[t])
        sg[t] = back(g, o).astype(BF16)
        og[t] = back(g, s).astype(BF16)
        return 0

    lax.fori_loop(0, STEPS, step, 0)
    cat = lambda ref: jnp.concatenate([ref[t] for t in range(STEPS)], axis=1)
    rows = lambda ref, j: jnp.concatenate([ref[t, pl.ds(j * J, J), :] for t in range(STEPS)], axis=1)
    for j in range(JS):
        part = dot_nt(cat(qs), rows(w, j)).astype(BF16)
        rout[2 * j], rout[2 * j + 1] = part[:, :B], part[:, B:]
    for j in range(JS):
        part = dot_nt(cat(sg), rows(ohs, j)).astype(BF16)
        lout[2 * j], lout[2 * j + 1] = part[:, :B], part[:, B:]
    part = dot_nt(cat(ohr), cat(og)).astype(BF16)
    for i in range(N):
        pout[i] = part[i * 16 : i * 16 + 16]


def bucket(lg, rg, rel, src, rid, tgt, neg):
    vm = pl.BlockSpec(memory_space=pltpu.VMEM)
    return pl.pallas_call(
        bucket_kernel,
        out_shape=(
            jax.ShapeDtypeStruct((N, W, B), BF16),
            jax.ShapeDtypeStruct((N, W, B), BF16),
            jax.ShapeDtypeStruct((N, 16, W), BF16),
        ),
        in_specs=[vm] * 7,
        out_specs=(vm,) * 3,
        scratch_shapes=[
            pltpu.VMEM((N * B, W), BF16),
            pltpu.VMEM((STEPS, N * B, T), BF16),
            pltpu.VMEM((STEPS, 256, T), BF16),
            pltpu.VMEM((STEPS, N * B, T), BF16),
            pltpu.VMEM((STEPS, W, T), BF16),
            pltpu.VMEM((STEPS, W, T), BF16),
            pltpu.VMEM((STEPS, W, T), BF16),
            pltpu.VMEM((2, N * B, B), F32),
        ],
        compiler_params=pltpu.CompilerParams(vmem_limit_bytes=VMEM_LIMIT),
        name="bucket_grads",
    )(lg, rg, rel, src, rid, tgt, neg)


def scatter_kernel(
    lp, rp, pp, lsum, rsum, psum,
    rb_half, rb, rstage, ybuf, cbuf, lb_half, lb, lstage, lx, lybuf,
    pbuf, prow, qbuf, qrow, fbuf, fown,
    zs, zr, cs, cr, xs, xr, ps, pr, qs, qr, fs, fr, ts, tr,
):
    me = Place()
    l, r = me.l, me.r
    zp, zm = me.left_at(1), me.left_at(-1)
    xp, xm = me.right_at(1), me.right_at(-1)
    yo, co = me.right_at(0, 1), me.right_at(0, 0, 1)
    l_other = me.left_at(0, 1)
    barrier = pltpu.get_barrier_semaphore()
    for i in range(1, N):
        pl.semaphore_signal(barrier, inc=1, device_id=(l, mod(r + i, N)), device_id_type=MESH)
        pl.semaphore_signal(barrier, inc=1, device_id=(mod(l + i, N), r), device_id_type=MESH)
    pl.semaphore_wait(barrier, 2 * (N - 1))

    sends = []

    def send(src, dst, s, d, left, right):
        copy = remote(src, dst, s, d, left, right)
        copy.start()
        sends.append(copy)

    def arrived(dst, d):
        remote(dst, dst, ts.at[2], d, l, co).wait_recv()

    low, high = pl.ds(0, LOW), pl.ds(LOW, HIGH)
    part = (low, high)
    zto, xto, sign = (zp, zm), (xp, xm), (1, -1)

    for k in (1, 0):
        a = me.left_at(4, k)
        for side in (0, 1):
            rows = pl.ds(0, LOW if side == 0 else HIGH)
            send(rp.at[a, part[side]], rb_half.at[side, k, rows], zs.at[side, 3, k], zr.at[side, 3, k], zto[side], r)
    for n, (x, k) in enumerate(((2, 0), (2, 1), (1, 0), (-1, 0), (1, 1), (-1, 1), (0, 0), (0, 1))):
        send(lp.at[me.right_at(x, k, 1)], cbuf.at[n], cs.at[n], cr.at[n], l, co)
    for i in range(1, N):
        to = mod(r + i, N)
        send(pp.at[to], pbuf.at[i], ps.at[i], pr.at[i], l, to)

    def chip_sum(n, x, k):
        arrived(cbuf.at[n], cr.at[n])
        return lp[me.right_at(x, k)].astype(F32) + cbuf[n].astype(F32)

    def right_step(d, k):
        a, b = me.left_at(d, k), me.left_at(-d, k)
        for side, at in ((0, a), (1, b)):
            mine = rp[at].astype(F32)
            if d == 3:
                rows = pl.ds(0, LOW if side == 0 else HIGH)
                arrived(rb_half.at[side, k, rows], zr.at[side, 3, k])
                got = rb_half[side, k, rows].astype(F32)
                if side == 0:
                    total = jnp.concatenate([mine[:LOW] + got, mine[LOW:]], axis=0)
                else:
                    total = jnp.concatenate([mine[:LOW], mine[LOW:] + got], axis=0)
            else:
                arrived(rb.at[side, d, k], zr.at[side, d, k])
                total = mine + rb[side, d, k].astype(F32)
            rstage[side, d - 1, k] = total.astype(BF16)
            send(rstage.at[side, d - 1, k], rb.at[side, d - 1, k], zs.at[side, d - 1, k], zr.at[side, d - 1, k], zto[side], r)

    for k in (1, 0):
        total = chip_sum(0 if k == 0 else 1, 2, k).astype(BF16)
        lstage[0, k] = total
        for side in (0, 1):
            rows = pl.ds(0, LOW if side == 0 else HIGH)
            send(lstage.at[0, k, part[side]], lb_half.at[side, k, rows], xs.at[side, 1, k], xr.at[side, 1, k], l, xto[side])
    right_step(3, 1)
    right_step(3, 0)

    total = pp[r].astype(F32)
    for i in range(1, N):
        arrived(pbuf.at[i], pr.at[i])
        total += pbuf[i].astype(F32)
    for i in range(N):
        prow[i] = total[i : i + 1]
    for i in range(1, N):
        to = mod(l + i, N)
        send(prow.at[to], qbuf.at[i], qs.at[i], qr.at[i], to, r)

    for k in (1, 0):
        for side in (0, 1):
            n = 2 + 2 * k + side
            total = chip_sum(n, sign[side], k)
            rows = pl.ds(0, LOW if side == 0 else HIGH)
            arrived(lb_half.at[side, k, rows], xr.at[side, 1, k])
            got = lb_half[side, k, rows].astype(F32)
            if side == 0:
                total = jnp.concatenate([total[:LOW] + got, total[LOW:]], axis=0)
            else:
                total = jnp.concatenate([total[:LOW], total[LOW:] + got], axis=0)
            lstage[1 + side, k] = total.astype(BF16)
            send(lstage.at[1 + side, k], lb.at[side, k], xs.at[side, 0, k], xr.at[side, 0, k], l, xto[side])
    right_step(2, 1)
    right_step(2, 0)

    total = prow[l]
    for i in range(1, N):
        arrived(qbuf.at[i], qr.at[i])
        total += qbuf[i]
    qrow[l] = total
    for i in range(1, N):
        to = mod(l + i, N)
        send(qrow.at[l], qrow.at[l], fs.at[i], fr.at[i], to, r)

    other = chip_sum(7, 0, 1)
    for side in (0, 1):
        arrived(lb.at[side, 1], xr.at[side, 0, 1])
        other += lb[side, 1].astype(F32)
    lx[...] = other.astype(BF16)
    send(lx, lybuf, ts.at[0], tr.at[0], l, yo)
    right_step(1, 1)
    total = chip_sum(6, 0, 0)
    for side in (0, 1):
        arrived(lb.at[side, 0], xr.at[side, 0, 0])
        total += lb[side, 0].astype(F32)
    lsum[...] = total
    right_step(1, 0)

    for i in range(1, N):
        arrived(qrow.at[mod(l - i, N)], fr.at[i])
    fown[...] = jnp.concatenate([qrow[i] for i in range(N)], axis=0)
    psum[r] = fown[...]
    for i in range(1, N):
        to = mod(r + i, N)
        send(fown, fbuf.at[i], pbs(ps, i), pbs(pr, i), l, to)

    other = rp[me.left_at(0, 1)].astype(F32)
    for side in (0, 1):
        arrived(rb.at[side, 0, 1], zr.at[side, 0, 1])
        other += rb[side, 0, 1].astype(F32)
    ybuf[0] = other.astype(BF16)
    send(ybuf.at[0], ybuf.at[1], ts.at[1], tr.at[1], l_other, r)
    arrived(lybuf, tr.at[0])
    lsum[...] += lybuf[...].astype(F32)
    total = rp[l].astype(F32)
    for side in (0, 1):
        arrived(rb.at[side, 0, 0], zr.at[side, 0, 0])
        total += rb[side, 0, 0].astype(F32)
    for i in range(1, N):
        arrived(fbuf.at[i], pbs(pr, i))
        psum[mod(r - i, N)] = fbuf[i]
    arrived(ybuf.at[1], tr.at[1])
    rsum[...] = total + ybuf[1].astype(F32)
    for copy in sends:
        copy.wait_send()


def pbs(ref, i):
    return ref.at[N + i]


def scatter(lp, rp, pp):
    vm = pl.BlockSpec(memory_space=pltpu.VMEM)
    dma = pltpu.SemaphoreType.DMA
    return pl.pallas_call(
        scatter_kernel,
        out_shape=(
            jax.ShapeDtypeStruct((W, B), F32),
            jax.ShapeDtypeStruct((W, B), F32),
            jax.ShapeDtypeStruct((N, 16, W), F32),
        ),
        in_specs=[vm] * 3,
        out_specs=(vm,) * 3,
        scratch_shapes=[
            pltpu.VMEM((2, 2, LOW, B), BF16),
            pltpu.VMEM((2, 3, 2, W, B), BF16),
            pltpu.VMEM((2, 3, 2, W, B), BF16),
            pltpu.VMEM((2, W, B), BF16),
            pltpu.VMEM((8, W, B), BF16),
            pltpu.VMEM((2, 2, LOW, B), BF16),
            pltpu.VMEM((2, 2, W, B), BF16),
            pltpu.VMEM((3, 2, W, B), BF16),
            pltpu.VMEM((W, B), BF16),
            pltpu.VMEM((W, B), BF16),
            pltpu.VMEM((N, 16, W), BF16),
            pltpu.VMEM((N, 1, W), F32),
            pltpu.VMEM((N, 1, W), F32),
            pltpu.VMEM((N, 1, W), F32),
            pltpu.VMEM((N, 16, W), F32),
            pltpu.VMEM((16, W), F32),
            dma((2, 4, 2)), dma((2, 4, 2)),
            dma((8,)), dma((8,)),
            dma((2, 2, 2)), dma((2, 2, 2)),
            dma((2 * N,)), dma((2 * N,)),
            dma((N,)), dma((N,)),
            dma((N,)), dma((N,)),
            dma((3,)), dma((2,)),
        ],
        compiler_params=pltpu.CompilerParams(collective_id=1, has_side_effects=True, vmem_limit_bytes=VMEM_LIMIT),
        name="scatter_grads",
    )(lp, rp, pp)


def adagrad(table, state, grad):
    state_new = state + jnp.mean(grad * grad, axis=-1)
    return (table - LEARN_RATE * grad / jnp.sqrt(state_new)[:, None], state_new)


def per_device(
    left_table,
    left_state,
    right_table,
    right_state,
    relation_table,
    relation_state,
    source_ids,
    target_ids,
    relation_ids,
    negative_ids,
):
    lt = left_table.astype(BF16).T
    rt = right_table.astype(BF16).T
    lg, rg, moved_table, moved_state = gather(lt, rt, right_table, right_state.reshape(1, B))
    rel = relation_table.astype(BF16).T
    src = source_ids.reshape(STEPS, 1, T)
    rid = relation_ids.reshape(STEPS, 1, T)
    tgt = target_ids.reshape(STEPS, 1, T)
    neg = negative_ids.reshape(2, 1, 1024)
    lp, rp, pp = bucket(lg, rg, rel, src, rid, tgt, neg)
    lsum, rsum, psum = scatter(lp, rp, pp)
    left_new, left_state_new = adagrad(left_table, left_state, lsum.T)
    right_new, right_state_new = adagrad(moved_table, moved_state.reshape(B), rsum.T)
    relation_new, relation_state_new = adagrad(relation_table, relation_state, psum.reshape(N * 16, W))
    return (left_new, left_state_new, right_new, right_state_new, relation_new, relation_state_new)


def solution(mesh):
    return jax.shard_map(
        per_device,
        mesh=mesh,
        in_specs=(
            P(("left", "right"), None),
            P(("left", "right")),
            P(("left", "right"), None),
            P(("left", "right")),
            P(),
            P(),
            P("left", "right", None),
            P("left", "right", None),
            P("left", "right", None),
            P("left", "right", None, None),
        ),
        out_specs=(
            P(("left", "right"), None),
            P(("left", "right")),
            P(("left", "right"), None),
            P(("left", "right")),
            P(),
            P(),
        ),
        check_vma=False,
    )
```

time: 662 us -> 111 us (0.17)
  waiting for transfers between devices: 572 us -> 0 us
  Pallas kernels: 0 us -> 94.6 us
  matrix products: 25.7 us -> 0 us
  local copies, waits for them, and re-layouts: 20.5 us -> 3.46 us
  between operations: 14 us -> 0.72 us
  starting transfers between devices: 8.91 us -> 0 us
    reduce_scatter x2 -> x0, waiting for transfers between devices: 232 us -> none  [the longest x1 169 us: per_device(): lax.psum_scatter(jnp.einsum('er,ed->rd', onehot, all_grads, preferred_ele...]
    psum x1 -> x0, waiting for transfers between devices: 230 us -> none  [per_device(): relation_total = lax.psum(relation_term, ('left', 'right'))]
    all_gather x2 -> x0, waiting for transfers between devices: 107 us -> none  [the longest x1 73 us: per_device(): lax.all_gather(moved_table.astype(jnp.bfloat16), 'left', axis=0, tiled=True)]
    pallas_call x0 -> x3, Pallas kernels: none -> 94.6 us  [the longest x1 38.7 us: scatter(): pl.pallas_call(scatter_kernel, out_shape=(jax.ShapeDtypeStruct((W, B), F3...]
    dot_general x9 -> x0, matrix products: 25.7 us -> none  [the longest x1 7.84 us: per_device(): jnp.einsum('er,ed->rd', onehot, all_grads, preferred_element_type=jnp.flo...]
    gather x2 -> x0, local copies, waits for them, and re-layouts: 13.2 us -> none  [per_device(): negative_rows = jnp.take(right_part, negative, axis=0)]
    ppermute x2 -> x0, starting transfers between devices: 8.53 us -> none  [from_behind(): lax.ppermute(value, axis, [(i, (i + by) % devices) for i in range(devices)])]
  transfers between devices with their start and end apart: 7 -> 0, of which waited for: 6 -> 0; matrix products, arithmetic and copies ran while one was open for 4% -> 0% of each run, Pallas kernels for 0% -> 0%
where the time goes in v1:
time: 111 us; the launch traced here: 110 us
  Pallas kernels  94.6 us (85%)
  other arithmetic  11.5 us (10%)
  local copies, waits for them, and re-layouts  3.46 us (3%)
    pallas_call x1, Pallas kernels, scatter(): pl.pallas_call(scatter_kernel, out_shape=(jax.ShapeDtypeStruct((W, B), F3...  38.7 us
    pallas_call x1, Pallas kernels, gather(): pl.pallas_call(gather_kernel, out_shape=(jax.ShapeDtypeStruct((N, W, B),...  33.9 us
    pallas_call x1, Pallas kernels, bucket(): pl.pallas_call(bucket_kernel, out_shape=(jax.ShapeDtypeStruct((N, W, B),...  22 us
    reduce_sum x3, other arithmetic, adagrad(): state_new = state + jnp.mean(grad * grad, axis=-1)  3.27 us
    sub x3, other arithmetic, adagrad(): return (table - LEARN_RATE * grad / jnp.sqrt(state_new)[:, None], state_new)  3.15 us

profile of v1, /device:TPU:1, one launch (start us, length us, event | category | flops | bytes accessed | tf_op | source)
XLA Modules:
  0.0 110.3 jit_solution(2987700453278459890)
XLA Ops:
  0.6 1.3 %reshape.51.neg = s32[2,1,1024]{2,1,0:T(1,128)} reshape(s32[1,1,2,1024]{3,2,1,0:T(2,128)} %param.19) | data formatting | bytes 16384 | tf_op jit(solution)/shard_map/reshape | solution.py:523
  1.9 1.7 %convert_bitcast_fusion.rel = bf16[400,256]{1,0:T(8,128)(2,1)} fusion(f32[256,400]{0,1:T(8,128)} %param.14), kind=kLoop, calls=%fused_computation.7 | loop fusion | flops 102400 | bytes 614400 | tf_op jit(solution)/shard_map/transpose | solution.py:519
  3.6 1.7 %convert_bitcast_fusion.1 = (bf16[400,128]{1,0:T(8,128)(2,1)}, bf16[400,128]{1,0:T(8,128)(2,1)}) fusion(f32[128,400]{0,1:T(8,128)} %param.12, f32[128,400]{0,1:T(8,128)} %param.10), kind=kLoop, calls=%fused_computation.8 | loop fusion | flops 102400 | bytes 614400 | tf_op jit(solution)/shard_map/transpose | solution.py:517
  5.4 1.8 %copy.16.table = f32[128,400]{1,0:T(8,128)} copy(f32[128,400]{0,1:T(8,128)} %param.12) | data formatting | bytes 409600 | tf_op args[2]
  7.1 33.9 %gather_parts.1 = (bf16[16,400,128]{2,1,0:T(8,128)(2,1)}, bf16[16,400,128]{2,1,0:T(8,128)(2,1)}, f32[128,400]{1,0:T(8,128)}, f32[1,128]{1,0:T(1,128)}) custom-call(bf16[400,128]{1,0:T(8,128)(2,1)} %get-tuple-element.35.lt, bf16[400,128]{1,0:T(8,128)(2,1)} %get-tuple-element.34.rt, f32[128,400]{1,0:T(8,128)} %copy.16.table, f32[1,128]{1,0:T(1,128)} %bitcast.22), custom_call_target="tpu_custom_call" | custom-call | tf_op jit(solution)/shard_map/gather_parts/pallas_call | solution.py:176
  41.1 22.0 %bucket_grads.1 = (bf16[16,400,128]{2,1,0:T(8,128)(2,1)}, bf16[16,400,128]{2,1,0:T(8,128)(2,1)}, bf16[16,16,400]{2,1,0:T(8,128)(2,1)}) custom-call(bf16[16,400,128]{2,1,0:T(8,128)(2,1)} %get-tuple-element.16.lg, bf16[16,400,128]{2,1,0:T(8,128)(2,1)} %get-tuple-element.17.rg, bf16[400,256]{1,0:T(8,128)(2,1)} %convert_bitcast_fusion.rel, ...), custom_call_target="tpu_custom_call" | custom-call | tf_op jit(solution)/shard_map/bucket_grads/pallas_call | solution.py:277
  63.1 38.7 %scatter_grads.1 = (f32[400,128]{1,0:T(8,128)}, f32[400,128]{1,0:T(8,128)}, f32[16,16,400]{2,1,0:T(8,128)}) custom-call(bf16[16,400,128]{2,1,0:T(8,128)(2,1)} %get-tuple-element.18.lp, bf16[16,400,128]{2,1,0:T(8,128)(2,1)} %get-tuple-element.19.rp, bf16[16,16,400]{2,1,0:T(8,128)(2,1)} %get-tuple-element.20.pp), custom_call_target="tpu_custom_call" | custom-call | tf_op jit(solution)/shard_map/scatter_grads/pallas_call | solution.py:460
  101.8 0.0 copy-start.4
  101.8 0.0 copy-start
  101.8 1.0 multiply_reduce_fusion.2
  102.9 1.0 multiply_reduce_fusion.1
  103.9 0.5 fusion.1
  104.4 0.5 fusion.2
  104.9 0.0 copy-done.1
  104.9 1.6 %bitcast_subtract_fusion.1 = f32[128,400]{0,1:T(8,128)} fusion(f32[128,400]{0,1:T(8,128)S(1)} %copy-done.1, f32[400,128]{1,0:T(8,128)} %get-tuple-element.21, f32[128]{0:T(128)S(1)} %get-tuple-element.30), kind=kLoop, calls=%fused_computation.4 | loop fusion | flops 153600 | bytes 614912 | tf_op jit(solution)/shard_map/sub | solution.py:501
  106.6 1.2 %multiply_reduce_fusion = (f32[16,16]{1,0:T(8,128)S(1)}, f32[16,16,400]{2,1,0:T(8,128)S(1)}) fusion(f32[16,16,400]{2,1,0:T(8,128)} %get-tuple-element.25), kind=kLoop, calls=%fused_computation | loop fusion | flops 306944 | bytes 820224 | tf_op jit(solution)/shard_map/reduce_sum | solution.py:500
  107.8 0.1 div.54
  107.9 0.2 copy.18
  108.0 0.0 copy-done.4
  108.1 0.6 fusion
  108.6 0.8 divide_subtract_fusion
  109.4 0.1 copy.17
  109.6 0.0 copy-done.2
  109.6 0.7 bitcast_subtract_fusion
  (10 shorter events, 0.0 us)
Async XLA Ops:
  63.1 40.8 %copy-start.6 = (f32[1,128]{1,0:T(1,128)S(1)}, f32[1,128]{1,0:T(1,128)}, u32[]{:S(2)}) copy-start(f32[1,128]{1,0:T(1,128)} %get-tuple-element.24) | copy-start | bytes 1540
  63.1 41.3 %copy-start.5 = (f32[128]{0:T(128)S(1)}, f32[128]{0:T(128)}, u32[]{:S(2)}) copy-start(f32[128]{0:T(128)} %param.11) | copy-start | bytes 1540
  63.1 41.9 %copy-start.1 = (f32[128,400]{0,1:T(8,128)S(1)}, f32[128,400]{0,1:T(8,128)}, u32[]{:S(2)}) copy-start(f32[128,400]{0,1:T(8,128)} %param.10) | copy-start | bytes 614404
  101.8 6.2 %copy-start.4 = (f32[256]{0:T(256)S(1)}, f32[256]{0:T(256)}, u32[]{:S(2)}) copy-start(f32[256]{0:T(256)} %param.15) | copy-start | bytes 3076
  101.8 6.8 %copy-start = (f32[256,400]{0,1:T(8,128)S(1)}, f32[256,400]{0,1:T(8,128)}, u32[]{:S(2)}) copy-start(f32[256,400]{0,1:T(8,128)} %param.14) | copy-start | bytes 1228804
  106.5 2.9 %copy-start.3 = (f32[128,400]{1,0:T(8,128)S(1)}, f32[128,400]{1,0:T(8,128)}, u32[]{:S(2)}) copy-start(f32[128,400]{1,0:T(8,128)} %get-tuple-element.22) | copy-start | bytes 614404
  106.5 3.0 %copy-start.2 = (f32[400,128]{1,0:T(8,128)S(1)}, f32[400,128]{1,0:T(8,128)}, u32[]{:S(2)}) copy-start(f32[400,128]{1,0:T(8,128)} %get-tuple-element.23) | copy-start | bytes 614404

commit v2 on v0

v2 whole, which is shorter than its diff:
```python
import functools

import jax
import jax.numpy as jnp
from jax import lax
from jax.experimental import pallas as pl
from jax.experimental.pallas import tpu as pltpu
from jax.sharding import PartitionSpec as P

LEARN_RATE = 0.1
NEG_WEIGHT = 0.03125
MESH = pl.DeviceIdType.MESH
F32, BF16 = jnp.float32, jnp.bfloat16

N = 16
W = 400
HALF = 200
B = 128
LOW = 208
HIGH = W - LOW
VMEM_LIMIT = 60 * 1024 * 1024


def mod(value, n):
    return lax.rem(value + 4 * n, n)


class Place:
    def __init__(self):
        self.l = lax.axis_index("left")
        self.r = lax.axis_index("right")
        self.z = lax.div(self.l, 2)
        self.h = lax.rem(self.l, 2)
        self.c = lax.rem(self.r, 2)
        self.x = lax.rem(lax.div(self.r, 2), 4)
        self.yl = lax.div(self.r, 8)

    def left_at(self, z, k=0):
        h = self.h if k == 0 else 1 - self.h
        return mod(self.z + z, 8) * 2 + h

    def right_at(self, x, k=0, other=0):
        yl = self.yl if k == 0 else 1 - self.yl
        c = self.c if other == 0 else 1 - self.c
        return (yl * 4 + mod(self.x + x, 4)) * 2 + c


def remote(src, dst, send, recv, left, right):
    return pltpu.make_async_remote_copy(
        src_ref=src,
        dst_ref=dst,
        send_sem=send,
        recv_sem=recv,
        device_id=(left, right),
        device_id_type=MESH,
    )


E = 1024
T = 256
TILES = tuple(slice(t * T, t * T + T) for t in range(E // T))
J = 256
LOWS, HIGHS = pl.ds(0, LOW), pl.ds(LOW, HIGH)
PART = (LOWS, HIGHS)


def one_hot(ids, first, rows):
    row = lax.broadcasted_iota(jnp.int32, (rows, ids.shape[-1]), 0)
    return row == ids - first


def ones(hit):
    return jnp.where(hit, 1.0, 0.0).astype(BF16)


def back(g, o):
    g_re, g_im, o_re, o_im = g[:HALF], g[HALF:], o[:HALF], o[HALF:]
    return jnp.concatenate([g_re * o_re + g_im * o_im, g_im * o_re - g_re * o_im], axis=0)


def dot(a, b):
    return lax.dot_general(a, b, (((1,), (0,)), ((), ())), preferred_element_type=F32)


def dot_nt(a, b):
    return lax.dot_general(a, b, (((1,), (1,)), ((), ())), preferred_element_type=F32)


def bucket_kernel(
    left, right, state, relation, src, rid, tgt, neg,
    lsum, rsum, psum, moved, moved_state,
    lt, rt, lg, rg, rn, rel, ohs, ohr, w, qs, ss_, os_, sg, og, mult, pos,
    rp, lp, pp,
    rb_half, rb, rstage, rfar, ybuf, cst, cbuf, lb_half, lb, lstage, lx, lybuf,
    pbuf, prow, qbuf, qrow, fbuf, fown,
    gs, gr, ls, lr, ms,
    zs, zr, cs, cr, xs, xr, ps, pr, qsm, qrm, fs, fr, ts, tr,
):
    me = Place()
    l, r = me.l, me.r
    ahead, behind = mod(r + 1, N), mod(r - 1, N)
    l_other = me.left_at(0, 1)
    zp, zm = me.left_at(1), me.left_at(-1)
    xp, xm = me.right_at(1), me.right_at(-1)
    yo, co = me.right_at(0, 1), me.right_at(0, 0, 1)
    barrier = pltpu.get_barrier_semaphore()

    def greet(a, b):
        pl.semaphore_signal(barrier, inc=1, device_id=(a, b), device_id_type=MESH)

    for i in range(1, N):
        greet(l, mod(r + i, N))
        greet(mod(l + i, N), r)
    greet(l_other, ahead)
    greet(l_other, behind)

    sends = []

    def send(src_ref, dst, s, d, a, b):
        copy = remote(src_ref, dst, s, d, a, b)
        copy.start()
        sends.append(copy)

    def arrived(dst, d):
        remote(dst, dst, ts.at[2], d, l, co).wait_recv()

    rt[...] = right[...].T.astype(BF16)
    lt[...] = left[...].T.astype(BF16)
    lg[r] = lt[...]
    rel[...] = relation[...].T.astype(BF16)
    ids = lambda ref, t: ref[0, :, TILES[t]]

    def counts(c, j):
        hit = jnp.where(one_hot(neg[0, 0, c : c + 1, :], j * J, J), NEG_WEIGHT, 0.0)
        mult[c, pl.ds(j * J, J), :] = jnp.broadcast_to(jnp.sum(hit, axis=1, keepdims=True), (J, B))

    def source_hot(j):
        ohs[pl.ds(j * J, J), :] = ones(one_hot(src[0], j * J, J))

    ohr[...] = ones(one_hot(rid[0], 0, 256))
    pos[...] = jnp.zeros_like(pos)
    pl.semaphore_wait(barrier, 2 * (N - 1) + 2)

    send(rt, rg.at[l], gs.at[0], gr.at[0], l, ahead)
    send(rt, rg.at[l], gs.at[1], gr.at[1], l_other, ahead)
    send(lt, lg.at[r], ls.at[0], lr.at[0], l, yo)
    send(lt, lg.at[r], ls.at[1], lr.at[1], l, xp)
    send(lt, lg.at[r], ls.at[2], lr.at[2], l, xm)
    send(lt, lg.at[r], ls.at[3], lr.at[3], l, co)

    def ring(d, k):
        i = 2 + 4 * (d - 1) + 2 * k
        a, b = me.left_at(-d, k), me.left_at(d, k)
        n = i + 4
        arrived(rg.at[a], gr.at[i])
        up, down = (rg.at[a], rg.at[b]) if d < 3 else (rg.at[a, LOWS], rg.at[b, HIGHS])
        send(up, up, gs.at[n], gr.at[n], zp, r)
        arrived(rg.at[b], gr.at[i + 1])
        send(down, down, gs.at[n + 1], gr.at[n + 1], zm, r)

    def across(k):
        a, b = me.right_at(-1, k), me.right_at(1, k)
        ra, rb_ = (1, 2) if k == 0 else (4, 5)
        i = 7 + 4 * k
        arrived(lg.at[a], lr.at[ra])
        send(lg.at[a, LOWS], lg.at[a, LOWS], ls.at[i], lr.at[i], l, xp)
        send(lg.at[a], lg.at[a], ls.at[i + 2], lr.at[i + 2], l, co)
        arrived(lg.at[b], lr.at[rb_])
        send(lg.at[b, HIGHS], lg.at[b, HIGHS], ls.at[i + 1], lr.at[i + 1], l, xm)
        send(lg.at[b], lg.at[b], ls.at[i + 3], lr.at[i + 3], l, co)

    def far(k):
        a = me.right_at(2, k)
        i = 7 + 4 * k
        arrived(lg.at[a, LOWS], lr.at[i])
        arrived(lg.at[a, HIGHS], lr.at[i + 1])
        send(lg.at[a], lg.at[a], ls.at[15 + k], lr.at[15 + k], l, co)

    for j in range(5):
        counts(0, j)
    arrived(rg.at[l], gr.at[0])
    send(rg.at[l], rg.at[l], gs.at[2], gr.at[2], zp, r)
    send(rg.at[l], rg.at[l], gs.at[3], gr.at[3], zm, r)
    arrived(lg.at[yo], lr.at[0])
    send(lg.at[yo], lg.at[yo], ls.at[4], lr.at[4], l, xp)
    send(lg.at[yo], lg.at[yo], ls.at[5], lr.at[5], l, xm)
    send(lg.at[yo], lg.at[yo], ls.at[6], lr.at[6], l, co)
    across(0)
    for j in range(5, 8):
        counts(0, j)
    arrived(rg.at[l_other], gr.at[1])
    send(rg.at[l_other], rg.at[l_other], gs.at[4], gr.at[4], zp, r)
    send(rg.at[l_other], rg.at[l_other], gs.at[5], gr.at[5], zm, r)
    send(right, moved, ms.at[0], ms.at[1], l, ahead)
    send(state, moved_state, ms.at[2], ms.at[3], l, ahead)
    for j in range(2):
        counts(1, j)
    ring(1, 0)
    across(1)
    for j in range(2, 8):
        counts(1, j)
    far(0)
    ring(1, 1)
    for j in range(4):
        source_hot(j)
    far(1)
    for j in range(4, 8):
        source_hot(j)
    for t in range(4):
        os_[:, TILES[t]] = dot(rel[...], ohr[:, TILES[t]])
    ring(2, 0)
    for x, k, i in ((0, 0, 3), (0, 1, 6), (-1, 0, 9), (1, 0, 10), (-1, 1, 13), (1, 1, 14), (2, 0, 15), (2, 1, 16)):
        arrived(lg.at[me.right_at(x, k, 1)], lr.at[i])

    lcat = lambda: jnp.concatenate([lg[i] for i in range(N)], axis=1)
    rcat = lambda: jnp.concatenate([rg[i] for i in range(N)], axis=1)

    def queries(t):
        s = dot(lcat(), ohs[:, TILES[t]])
        o = os_[:, TILES[t]]
        ss_[:, TILES[t]] = s
        s_re, s_im, o_re, o_im = s[:HALF], s[HALF:], o[:HALF], o[HALF:]
        q = jnp.concatenate([s_re * o_re - s_im * o_im, s_re * o_im + s_im * o_re], axis=0)
        qs[:, TILES[t]] = q.astype(BF16)

    def rows_of(d):
        return pl.multiple_of(mod(me.z + d, 8) * J, J)

    def turn(d):
        zi = mod(me.z + d, 8)
        first = rows_of(d)
        rn[pl.ds(first, B), :] = rg[2 * zi].T
        rn[pl.ds(first + B, B), :] = rg[2 * zi + 1].T

    def scores(d):
        first = rows_of(d)
        for t in range(4):
            score = dot(rn[pl.ds(first, J), :], qs[:, TILES[t]])
            hit = one_hot(ids(tgt, t), first, J)
            found = jnp.where(hit, score, 0.0)
            pos[:, TILES[t]] += jnp.sum(found.reshape(J // 8, 8, T), axis=0)
            m = mult[t // 2, pl.ds(first, J), :]
            m = jnp.concatenate([m, m], axis=1)
            w[pl.ds(first, J), TILES[t]] = (jax.nn.sigmoid(score) * m).astype(BF16)

    turn(0)
    turn(1)
    turn(-1)
    queries(0)
    queries(1)
    ring(2, 1)
    queries(2)
    queries(3)
    scores(0)
    ring(3, 0)
    scores(1)
    scores(-1)
    turn(2)
    turn(-2)
    ring(3, 1)
    scores(2)
    scores(-2)
    turn(3)
    turn(-3)
    scores(3)
    scores(-3)
    for k in (0, 1):
        a = me.left_at(4, k)
        arrived(rg.at[a, LOWS], gr.at[14 + 2 * k])
        arrived(rg.at[a, HIGHS], gr.at[15 + 2 * k])
    turn(4)
    scores(4)

    def pos_grads(t):
        positive = jnp.sum(pos[:, TILES[t]], axis=0, keepdims=True)
        return -jax.nn.sigmoid(-positive)

    grads = [pos_grads(t) for t in range(4)]

    def weights(d):
        first = rows_of(d)
        for t in range(4):
            hit = one_hot(ids(tgt, t), first, J)
            old = w[pl.ds(first, J), TILES[t]].astype(F32)
            w[pl.ds(first, J), TILES[t]] = (old + jnp.where(hit, grads[t], 0.0)).astype(BF16)

    def right_grad(d):
        zi = mod(me.z + d, 8)
        part = dot_nt(qs[...], w[pl.ds(rows_of(d), J), :])
        rp[2 * zi] = part[:, :B]
        rp[2 * zi + 1] = part[:, B:]

    zto, xto, sign = (zp, zm), (xp, xm), (1, -1)

    weights(4)
    right_grad(4)
    for k in (1, 0):
        rfar[k] = rp[me.left_at(4, k)].astype(BF16)
    for k in (1, 0):
        for side in (0, 1):
            rows = pl.ds(0, LOW if side == 0 else HIGH)
            send(rfar.at[k, PART[side]], rb_half.at[side, k, rows], zs.at[side, 3, k], zr.at[side, 3, k], zto[side], r)
    weights(3)
    right_grad(3)
    weights(-3)
    right_grad(-3)
    for d in (2, -2, 1, -1, 0):
        weights(d)

    def right_step(d, k):
        for side, at in ((0, me.left_at(d, k)), (1, me.left_at(-d, k))):
            mine = rp[at]
            if d == 3:
                rows = pl.ds(0, LOW if side == 0 else HIGH)
                arrived(rb_half.at[side, k, rows], zr.at[side, 3, k])
                got = rb_half[side, k, rows].astype(F32)
                if side == 0:
                    total = jnp.concatenate([mine[:LOW] + got, mine[LOW:]], axis=0)
                else:
                    total = jnp.concatenate([mine[:LOW], mine[LOW:] + got], axis=0)
            else:
                arrived(rb.at[side, d, k], zr.at[side, d, k])
                total = mine + rb[side, d, k].astype(F32)
            rstage[side, d - 1, k] = total.astype(BF16)
            send(rstage.at[side, d - 1, k], rb.at[side, d - 1, k], zs.at[side, d - 1, k], zr.at[side, d - 1, k], zto[side], r)

    def query_grads(t):
        g = dot(rcat(), w[:, TILES[t]])
        sg[:, TILES[t]] = back(g, os_[:, TILES[t]]).astype(BF16)
        og[:, TILES[t]] = back(g, ss_[:, TILES[t]]).astype(BF16)

    query_grads(0)
    right_step(3, 1)
    right_step(3, 0)
    for t in range(1, 4):
        query_grads(t)
    part = dot_nt(ohr[...], og[...]).astype(BF16)
    for i in range(N):
        pp[i] = part[i * 16 : i * 16 + 16]
    for i in range(1, N):
        to = mod(r + i, N)
        send(pp.at[to], pbuf.at[i], ps.at[i], pr.at[i], l, to)
    right_grad(2)
    right_grad(-2)

    order = ((2, 0), (2, 1), (1, 0), (-1, 0), (1, 1), (-1, 1), (0, 0), (0, 1))

    def left_grad(n):
        x, k = order[n]
        g = lax.div(me.right_at(x, k), 2)
        part = dot_nt(sg[...], ohs[pl.ds(pl.multiple_of(g * J, J), J), :])
        lp[2 * g] = part[:, :B]
        lp[2 * g + 1] = part[:, B:]
        cst[n] = lp[me.right_at(x, k, 1)].astype(BF16)
        send(cst.at[n], cbuf.at[n], cs.at[n], cr.at[n], l, co)

    def chip_sum(n):
        x, k = order[n]
        arrived(cbuf.at[n], cr.at[n])
        return lp[me.right_at(x, k)] + cbuf[n].astype(F32)

    for n in range(6):
        left_grad(n)
    right_step(2, 1)
    right_step(2, 0)
    for k in (1, 0):
        lstage[0, k] = chip_sum(k).astype(BF16)
        for side in (0, 1):
            rows = pl.ds(0, LOW if side == 0 else HIGH)
            send(lstage.at[0, k, PART[side]], lb_half.at[side, k, rows], xs.at[side, 1, k], xr.at[side, 1, k], l, xto[side])
    left_grad(6)
    left_grad(7)
    right_grad(1)
    right_grad(-1)
    right_grad(0)

    total = pp[r].astype(F32)
    for i in range(1, N):
        arrived(pbuf.at[i], pr.at[i])
        total += pbuf[i].astype(F32)
    for i in range(N):
        prow[i] = total[i : i + 1]
    for i in range(1, N):
        to = mod(l + i, N)
        send(prow.at[to], qbuf.at[i], qsm.at[i], qrm.at[i], to, r)

    right_step(1, 1)
    for k in (1, 0):
        for side in (0, 1):
            total = chip_sum(2 + 2 * k + side)
            rows = pl.ds(0, LOW if side == 0 else HIGH)
            arrived(lb_half.at[side, k, rows], xr.at[side, 1, k])
            got = lb_half[side, k, rows].astype(F32)
            if side == 0:
                total = jnp.concatenate([total[:LOW] + got, total[LOW:]], axis=0)
            else:
                total = jnp.concatenate([total[:LOW], total[LOW:] + got], axis=0)
            lstage[1 + side, k] = total.astype(BF16)
            send(lstage.at[1 + side, k], lb.at[side, k], xs.at[side, 0, k], xr.at[side, 0, k], l, xto[side])
    right_step(1, 0)

    total = prow[l]
    for i in range(1, N):
        arrived(qbuf.at[i], qrm.at[i])
        total += qbuf[i]
    qrow[l] = total
    for i in range(1, N):
        to = mod(l + i, N)
        send(qrow.at[l], qrow.at[l], fs.at[i], fr.at[i], to, r)

    other = rp[me.left_at(0, 1)]
    for side in (0, 1):
        arrived(rb.at[side, 0, 1], zr.at[side, 0, 1])
        other += rb[side, 0, 1].astype(F32)
    ybuf[0] = other.astype(BF16)
    send(ybuf.at[0], ybuf.at[1], ts.at[1], tr.at[1], l_other, r)
    other = chip_sum(7)
    for side in (0, 1):
        arrived(lb.at[side, 1], xr.at[side, 0, 1])
        other += lb[side, 1].astype(F32)
    lx[...] = other.astype(BF16)
    send(lx, lybuf, ts.at[0], tr.at[0], l, yo)
    total = chip_sum(6)
    for side in (0, 1):
        arrived(lb.at[side, 0], xr.at[side, 0, 0])
        total += lb[side, 0].astype(F32)
    lsum[...] = total

    for i in range(1, N):
        arrived(qrow.at[mod(l - i, N)], fr.at[i])
    fown[...] = jnp.concatenate([qrow[i] for i in range(N)], axis=0)
    psum[r] = fown[...]
    for i in range(1, N):
        to = mod(r + i, N)
        send(fown, fbuf.at[i], ps.at[N + i], pr.at[N + i], l, to)

    total = rp[l]
    for side in (0, 1):
        arrived(rb.at[side, 0, 0], zr.at[side, 0, 0])
        total += rb[side, 0, 0].astype(F32)
    arrived(ybuf.at[1], tr.at[1])
    rsum[...] = total + ybuf[1].astype(F32)
    arrived(lybuf, tr.at[0])
    lsum[...] += lybuf[...].astype(F32)
    arrived(moved, ms.at[1])
    arrived(moved_state, ms.at[3])
    for i in range(1, N):
        arrived(fbuf.at[i], pr.at[N + i])
        psum[mod(r - i, N)] = fbuf[i]
    for copy in sends:
        copy.wait_send()


def bucket(left, right, state, relation, src, rid, tgt, neg):
    vm = pl.BlockSpec(memory_space=pltpu.VMEM)
    dma = pltpu.SemaphoreType.DMA
    blocks = pltpu.VMEM((N, W, B), BF16)
    return pl.pallas_call(
        bucket_kernel,
        out_shape=(
            jax.ShapeDtypeStruct((W, B), F32),
            jax.ShapeDtypeStruct((W, B), F32),
            jax.ShapeDtypeStruct((N, 16, W), F32),
            jax.ShapeDtypeStruct((B, W), F32),
            jax.ShapeDtypeStruct((1, B), F32),
        ),
        in_specs=[vm] * 8,
        out_specs=(vm,) * 5,
        scratch_shapes=[
            pltpu.VMEM((W, B), BF16),
            pltpu.VMEM((W, B), BF16),
            blocks,
            blocks,
            pltpu.VMEM((N * B, W), BF16),
            pltpu.VMEM((W, 256), BF16),
            pltpu.VMEM((N * B, E), BF16),
            pltpu.VMEM((256, E), BF16),
            pltpu.VMEM((N * B, E), BF16),
            pltpu.VMEM((W, E), BF16),
            pltpu.VMEM((W, E), F32),
            pltpu.VMEM((W, E), F32),
            pltpu.VMEM((W, E), BF16),
            pltpu.VMEM((W, E), BF16),
            pltpu.VMEM((2, N * B, B), F32),
            pltpu.VMEM((8, E), F32),
            pltpu.VMEM((N, W, B), F32),
            pltpu.VMEM((N, W, B), F32),
            pltpu.VMEM((N, 16, W), BF16),
            pltpu.VMEM((2, 2, LOW, B), BF16),
            pltpu.VMEM((2, 3, 2, W, B), BF16),
            pltpu.VMEM((2, 3, 2, W, B), BF16),
            pltpu.VMEM((2, W, B), BF16),
            pltpu.VMEM((2, W, B), BF16),
            pltpu.VMEM((8, W, B), BF16),
            pltpu.VMEM((8, W, B), BF16),
            pltpu.VMEM((2, 2, LOW, B), BF16),
            pltpu.VMEM((2, 2, W, B), BF16),
            pltpu.VMEM((3, 2, W, B), BF16),
            pltpu.VMEM((W, B), BF16),
            pltpu.VMEM((W, B), BF16),
            pltpu.VMEM((N, 16, W), BF16),
            pltpu.VMEM((N, 1, W), F32),
            pltpu.VMEM((N, 1, W), F32),
            pltpu.VMEM((N, 1, W), F32),
            pltpu.VMEM((N, 16, W), F32),
            pltpu.VMEM((16, W), F32),
            dma((18,)), dma((18,)), dma((17,)), dma((17,)), dma((4,)),
            dma((2, 4, 2)), dma((2, 4, 2)),
            dma((8,)), dma((8,)),
            dma((2, 2, 2)), dma((2, 2, 2)),
            dma((2 * N,)), dma((2 * N,)),
            dma((N,)), dma((N,)),
            dma((N,)), dma((N,)),
            dma((3,)), dma((2,)),
        ],
        compiler_params=pltpu.CompilerParams(collective_id=0, has_side_effects=True, vmem_limit_bytes=VMEM_LIMIT),
        name="bucket_round",
    )(left, right, state, relation, src, rid, tgt, neg)


def update_kernel(left, left_state, lsum, moved, moved_state, rsum, rel, rel_state, psum, lo, lso, ro, rso, po, pso):
    for table, state, grad, out, state_out in (
        (left, left_state, lsum, lo, lso),
        (moved, moved_state, rsum, ro, rso),
    ):
        g = grad[...]
        new = state[...] + jnp.sum(g * g, axis=0, keepdims=True) * (1.0 / W)
        state_out[...] = new
        out[...] = table[...] - (LEARN_RATE * g / jnp.sqrt(new)).T
    g = psum[...].reshape(256, W)
    mean = jnp.sum(g * g, axis=1, keepdims=True) * (1.0 / W)
    state = jnp.broadcast_to(rel_state[...], (8, 256)).T[:, :1]
    new = state + mean
    po[...] = rel[...] - LEARN_RATE * g / jnp.sqrt(new)
    pso[...] = jnp.broadcast_to(new, (256, 8)).T[:1]


def update(*args):
    vm = pl.BlockSpec(memory_space=pltpu.VMEM)
    return pl.pallas_call(
        update_kernel,
        out_shape=(
            jax.ShapeDtypeStruct((B, W), F32),
            jax.ShapeDtypeStruct((1, B), F32),
            jax.ShapeDtypeStruct((B, W), F32),
            jax.ShapeDtypeStruct((1, B), F32),
            jax.ShapeDtypeStruct((256, W), F32),
            jax.ShapeDtypeStruct((1, 256), F32),
        ),
        in_specs=[vm] * 9,
        out_specs=(vm,) * 6,
        name="update_tables",
    )(*args)


def per_device(
    left_table,
    left_state,
    right_table,
    right_state,
    relation_table,
    relation_state,
    source_ids,
    target_ids,
    relation_ids,
    negative_ids,
):
    row = lambda state: state.reshape(1, -1)
    lsum, rsum, psum, moved, moved_state = bucket(
        left_table, right_table, row(right_state), relation_table, source_ids, relation_ids, target_ids, negative_ids
    )
    left_new, left_state_new, right_new, right_state_new, relation_new, relation_state_new = update(
        left_table, row(left_state), lsum, moved, moved_state, rsum, relation_table, row(relation_state), psum
    )
    flat = lambda state: state.reshape(-1)
    return (left_new, flat(left_state_new), right_new, flat(right_state_new), relation_new, flat(relation_state_new))


def solution(mesh):
    return jax.shard_map(
        per_device,
        mesh=mesh,
        in_specs=(
            P(("left", "right"), None),
            P(("left", "right")),
            P(("left", "right"), None),
            P(("left", "right")),
            P(),
            P(),
            P("left", "right", None),
            P("left", "right", None),
            P("left", "right", None),
            P("left", "right", None, None),
        ),
        out_specs=(
            P(("left", "right"), None),
            P(("left", "right")),
            P(("left", "right"), None),
            P(("left", "right")),
            P(),
            P(),
        ),
        check_vma=False,
    )
```

time: 662 us -> 88.8 us (0.13)
  waiting for transfers between devices: 572 us -> 0 us
  Pallas kernels: 0 us -> 79.8 us
  matrix products: 25.7 us -> 0 us
  other arithmetic: 16.3 us -> 0 us
  between operations: 14 us -> 0.66 us
  local copies, waits for them, and re-layouts: 20.5 us -> 8.18 us
  starting transfers between devices: 8.91 us -> 0 us
    reduce_scatter x2 -> x0, waiting for transfers between devices: 232 us -> none  [the longest x1 169 us: per_device(): lax.psum_scatter(jnp.einsum('er,ed->rd', onehot, all_grads, preferred_ele...]
    psum x1 -> x0, waiting for transfers between devices: 230 us -> none  [per_device(): relation_total = lax.psum(relation_term, ('left', 'right'))]
    all_gather x2 -> x0, waiting for transfers between devices: 107 us -> none  [the longest x1 73 us: per_device(): lax.all_gather(moved_table.astype(jnp.bfloat16), 'left', axis=0, tiled=True)]
    pallas_call x0 -> x2, Pallas kernels: none -> 79.8 us  [the longest x1 76.9 us: bucket(): pl.pallas_call(bucket_kernel, out_shape=(jax.ShapeDtypeStruct((W, B), F32...]
    dot_general x9 -> x0, matrix products: 25.7 us -> none  [the longest x1 7.84 us: per_device(): jnp.einsum('er,ed->rd', onehot, all_grads, preferred_element_type=jnp.flo...]
    gather x2 -> x0, local copies, waits for them, and re-layouts: 13.2 us -> none  [per_device(): negative_rows = jnp.take(right_part, negative, axis=0)]
    ppermute x2 -> x0, starting transfers between devices: 8.53 us -> none  [from_behind(): lax.ppermute(value, axis, [(i, (i + by) % devices) for i in range(devices)])]
  transfers between devices with their start and end apart: 7 -> 0, of which waited for: 6 -> 0; matrix products, arithmetic and copies ran while one was open for 4% -> 0% of each run, Pallas kernels for 0% -> 0%
where the time goes in v2:
time: 88.8 us; the launch traced here: 88.6 us
  Pallas kernels  79.8 us (90%)
  local copies, waits for them, and re-layouts  8.18 us (9%)
    pallas_call x1, Pallas kernels, bucket(): pl.pallas_call(bucket_kernel, out_shape=(jax.ShapeDtypeStruct((W, B), F32...  76.9 us
    unnamed x12, local copies, waits for them, and re-layouts  8.18 us
    pallas_call x1, Pallas kernels, update(): pl.pallas_call(update_kernel, out_shape=(jax.ShapeDtypeStruct((B, W), F32...  2.9 us

profile of v2, /device:TPU:1, one launch (start us, length us, event | category | flops | bytes accessed | tf_op | source)
XLA Modules:
  0.0 88.6 jit_solution(2047632499682774384)
XLA Ops:
  0.6 0.0 copy-start.2
  0.6 0.0 copy-start.1
  0.7 1.8 %copy.19.left = f32[128,400]{1,0:T(8,128)} copy(f32[128,400]{0,1:T(8,128)} %param.10) | data formatting | bytes 409600 | tf_op args[0]
  2.5 0.0 copy-done.2
  2.5 0.8 copy.17.right
  3.3 0.0 copy-done.1
  3.3 1.0 %copy.18.relation.rel = f32[256,400]{1,0:T(8,128)} copy(f32[256,400]{0,1:T(8,128)S(1)} %copy-done.1) | data formatting | bytes 819200 | tf_op args[4]
  4.3 76.9 %bucket_round.1 = (f32[400,128]{1,0:T(8,128)}, f32[400,128]{1,0:T(8,128)}, f32[16,16,400]{2,1,0:T(8,128)}, f32[128,400]{1,0:T(8,128)}, f32[1,128]{1,0:T(1,128)}) custom-call(f32[128,400]{1,0:T(8,128)} %copy.19.left, f32[128,400]{1,0:T(8,128)} %copy.17.right, f32[1,128]{1,0:T(1,128)} %bitcast.7, f32[256,400]{1,0:T(8,128)} %copy.18.relation.rel, ...), custom_call_target="tpu_custom_call" | custom-call | tf_op jit(solution)/shard_map/bucket_round/pallas_call | solution.py:458
  81.2 2.9 %update_tables.1 = (f32[128,400]{1,0:T(8,128)}, f32[1,128]{1,0:T(1,128)}, f32[128,400]{1,0:T(8,128)}, f32[1,128]{1,0:T(1,128)}, f32[256,400]{1,0:T(8,128)}, /*index=5*/f32[1,256]{1,0:T(1,128)}) custom-call(f32[128,400]{1,0:T(8,128)} %copy.19.left, f32[1,128]{1,0:T(1,128)} %bitcast.8, f32[400,128]{1,0:T(8,128)} %get-tuple-element.17.lsum, ...), custom_call_target="tpu_custom_call" | custom-call | tf_op jit(solution)/shard_map/update_tables/pallas_call | solution.py:540
  84.1 0.0 copy-start
  84.1 1.8 %copy.21 = f32[128,400]{0,1:T(8,128)} copy(f32[128,400]{1,0:T(8,128)} %get-tuple-element.28) | data formatting | bytes 409600
  85.9 1.8 %copy.22 = f32[128,400]{0,1:T(8,128)} copy(f32[128,400]{1,0:T(8,128)} %get-tuple-element.30) | data formatting | bytes 409600
  87.7 0.0 copy-done
  87.7 0.9 %copy.23 = f32[256,400]{0,1:T(8,128)} copy(f32[256,400]{1,0:T(8,128)S(1)} %copy-done) | data formatting | bytes 819200
Async XLA Ops:
  0.6 1.9 %copy-start.2 = (f32[128,400]{0,1:T(8,128)S(1)}, f32[128,400]{0,1:T(8,128)}, u32[]{:S(2)}) copy-start(f32[128,400]{0,1:T(8,128)} %param.12) | copy-start | bytes 614404
  0.6 2.7 %copy-start.1 = (f32[256,400]{0,1:T(8,128)S(1)}, f32[256,400]{0,1:T(8,128)}, u32[]{:S(2)}) copy-start(f32[256,400]{0,1:T(8,128)} %param.14) | copy-start | bytes 1228804
  84.1 3.6 %copy-start = (f32[256,400]{1,0:T(8,128)S(1)}, f32[256,400]{1,0:T(8,128)}, u32[]{:S(2)}) copy-start(f32[256,400]{1,0:T(8,128)} %get-tuple-element.32) | copy-start | bytes 1228804

commit v3 on v2

--- a/solution.py
+++ b/solution.py
@@ -89,8 +89,8 @@
 def bucket_kernel(
     left, right, state, relation, src, rid, tgt, neg,
     lsum, rsum, psum, moved, moved_state,
-    lt, rt, lg, rg, rn, rel, ohs, ohr, w, qs, ss_, os_, sg, og, mult, pos,
-    rp, lp, pp,
+    lt, rt, lg, rg, rn, rel, ohs, ohr, w, qs, ss_, os_, sg, og, mult,
+    rp, lp, pp, oht, tt, gq, qf, tg,
     rb_half, rb, rstage, rfar, ybuf, cst, cbuf, lb_half, lb, lstage, lx, lybuf,
     pbuf, prow, qbuf, qrow, fbuf, fown,
     gs, gr, ls, lr, ms,
@@ -108,11 +108,10 @@
     def greet(a, b):
         pl.semaphore_signal(barrier, inc=1, device_id=(a, b), device_id_type=MESH)
 
-    for i in range(1, N):
-        greet(l, mod(r + i, N))
-        greet(mod(l + i, N), r)
-    greet(l_other, ahead)
-    greet(l_other, behind)
+    peers = [(a, b) for a in (l_other, zp, zm) for b in (ahead, behind)]
+    peers += [(l, mod(r + i, N)) for i in range(1, N)] + [(mod(l + i, N), r) for i in range(1, N)]
+    for a, b in peers:
+        greet(a, b)
 
     sends = []
 
@@ -124,10 +123,10 @@
     def arrived(dst, d):
         remote(dst, dst, ts.at[2], d, l, co).wait_recv()
 
-    rt[...] = right[...].T.astype(BF16)
-    lt[...] = left[...].T.astype(BF16)
+    rt[...] = right[...].astype(BF16)
+    lt[...] = left[...].astype(BF16)
     lg[r] = lt[...]
-    rel[...] = relation[...].T.astype(BF16)
+    rel[...] = relation[...].astype(BF16)
     ids = lambda ref, t: ref[0, :, TILES[t]]
 
     def counts(c, j):
@@ -136,13 +135,15 @@
 
     def source_hot(j):
         ohs[pl.ds(j * J, J), :] = ones(one_hot(src[0], j * J, J))
+        oht[pl.ds(j * J, J), :] = ones(one_hot(tgt[0], j * J, J))
 
     ohr[...] = ones(one_hot(rid[0], 0, 256))
-    pos[...] = jnp.zeros_like(pos)
-    pl.semaphore_wait(barrier, 2 * (N - 1) + 2)
-
+    pl.semaphore_wait(barrier, len(peers))
+
+    send(rt, rg.at[l], gs.at[1], gr.at[1], l_other, ahead)
+    send(rt, rg.at[l], gs.at[2], gr.at[2], zp, ahead)
+    send(rt, rg.at[l], gs.at[3], gr.at[3], zm, ahead)
     send(rt, rg.at[l], gs.at[0], gr.at[0], l, ahead)
-    send(rt, rg.at[l], gs.at[1], gr.at[1], l_other, ahead)
     send(lt, lg.at[r], ls.at[0], lr.at[0], l, yo)
     send(lt, lg.at[r], ls.at[1], lr.at[1], l, xp)
     send(lt, lg.at[r], ls.at[2], lr.at[2], l, xm)
@@ -176,44 +177,58 @@
         arrived(lg.at[a, HIGHS], lr.at[i + 1])
         send(lg.at[a], lg.at[a], ls.at[15 + k], lr.at[15 + k], l, co)
 
-    for j in range(5):
+    for j in range(4):
         counts(0, j)
-    arrived(rg.at[l], gr.at[0])
-    send(rg.at[l], rg.at[l], gs.at[2], gr.at[2], zp, r)
-    send(rg.at[l], rg.at[l], gs.at[3], gr.at[3], zm, r)
     arrived(lg.at[yo], lr.at[0])
     send(lg.at[yo], lg.at[yo], ls.at[4], lr.at[4], l, xp)
     send(lg.at[yo], lg.at[yo], ls.at[5], lr.at[5], l, xm)
     send(lg.at[yo], lg.at[yo], ls.at[6], lr.at[6], l, co)
     across(0)
-    for j in range(5, 8):
+    for j in range(4, 6):
         counts(0, j)
     arrived(rg.at[l_other], gr.at[1])
     send(rg.at[l_other], rg.at[l_other], gs.at[4], gr.at[4], zp, r)
     send(rg.at[l_other], rg.at[l_other], gs.at[5], gr.at[5], zm, r)
-    send(right, moved, ms.at[0], ms.at[1], l, ahead)
-    send(state, moved_state, ms.at[2], ms.at[3], l, ahead)
-    for j in range(2):
+    counts(0, 6)
+    counts(0, 7)
+    ring(1, 0)
+    counts(1, 0)
+    across(1)
+    for j in range(1, 5):
         counts(1, j)
-    ring(1, 0)
-    across(1)
-    for j in range(2, 8):
+    ring(1, 1)
+    for j in range(5, 8):
         counts(1, j)
     far(0)
-    ring(1, 1)
-    for j in range(4):
+    for j in range(3):
         source_hot(j)
+    ring(2, 0)
     far(1)
-    for j in range(4, 8):
+    for j in range(3, 8):
         source_hot(j)
     for t in range(4):
         os_[:, TILES[t]] = dot(rel[...], ohr[:, TILES[t]])
-    ring(2, 0)
-    for x, k, i in ((0, 0, 3), (0, 1, 6), (-1, 0, 9), (1, 0, 10), (-1, 1, 13), (1, 1, 14), (2, 0, 15), (2, 1, 16)):
-        arrived(lg.at[me.right_at(x, k, 1)], lr.at[i])
 
     lcat = lambda: jnp.concatenate([lg[i] for i in range(N)], axis=1)
-    rcat = lambda: jnp.concatenate([rg[i] for i in range(N)], axis=1)
+
+    def slots_of(*ds):
+        zs_ = [mod(me.z + d, 8) for d in ds]
+        return jnp.concatenate([rg[2 * zi + h] for zi in zs_ for h in (0, 1)], axis=1)
+
+    def rows_from(ref, t, *ds):
+        return jnp.concatenate([ref[pl.ds(rows_of(d), J), TILES[t]] for d in ds], axis=0)
+
+    def gather_targets(*ds):
+        blocks = slots_of(*ds)
+        for t in range(4):
+            part = dot(blocks, rows_from(oht, t, *ds))
+            tt[:, TILES[t]] = part if 0 in ds else tt[:, TILES[t]] + part
+
+    def from_negatives(*ds):
+        blocks = slots_of(*ds)
+        for t in range(4):
+            part = dot(blocks, rows_from(w, t, *ds))
+            gq[:, TILES[t]] = part if 0 in ds else gq[:, TILES[t]] + part
 
     def queries(t):
         s = dot(lcat(), ohs[:, TILES[t]])
@@ -221,6 +236,7 @@
         ss_[:, TILES[t]] = s
         s_re, s_im, o_re, o_im = s[:HALF], s[HALF:], o[:HALF], o[HALF:]
         q = jnp.concatenate([s_re * o_re - s_im * o_im, s_re * o_im + s_im * o_re], axis=0)
+        qf[:, TILES[t]] = q
         qs[:, TILES[t]] = q.astype(BF16)
 
     def rows_of(d):
@@ -236,63 +252,73 @@
         first = rows_of(d)
         for t in range(4):
             score = dot(rn[pl.ds(first, J), :], qs[:, TILES[t]])
-            hit = one_hot(ids(tgt, t), first, J)
-            found = jnp.where(hit, score, 0.0)
-            pos[:, TILES[t]] += jnp.sum(found.reshape(J // 8, 8, T), axis=0)
             m = mult[t // 2, pl.ds(first, J), :]
             m = jnp.concatenate([m, m], axis=1)
             w[pl.ds(first, J), TILES[t]] = (jax.nn.sigmoid(score) * m).astype(BF16)
 
+    arrived(rg.at[l], gr.at[0])
     turn(0)
-    turn(1)
-    turn(-1)
+    gather_targets(0)
+    for x, k, i in ((0, 0, 3), (0, 1, 6), (-1, 0, 9), (1, 0, 10), (-1, 1, 13), (1, 1, 14), (2, 0, 15), (2, 1, 16)):
+        arrived(lg.at[me.right_at(x, k, 1)], lr.at[i])
     queries(0)
     queries(1)
     ring(2, 1)
+    send(right, moved, ms.at[0], ms.at[1], l, ahead)
+    send(state, moved_state, ms.at[2], ms.at[3], l, ahead)
     queries(2)
     queries(3)
     scores(0)
+    from_negatives(0)
+    turn(1)
+    turn(-1)
     ring(3, 0)
+    gather_targets(1, -1)
     scores(1)
     scores(-1)
+    from_negatives(1, -1)
+    ring(3, 1)
     turn(2)
     turn(-2)
-    ring(3, 1)
+    gather_targets(2, -2)
     scores(2)
     scores(-2)
+    from_negatives(2, -2)
     turn(3)
     turn(-3)
+    gather_targets(3, -3)
     scores(3)
     scores(-3)
+    from_negatives(3, -3)
     for k in (0, 1):
         a = me.left_at(4, k)
         arrived(rg.at[a, LOWS], gr.at[14 + 2 * k])
         arrived(rg.at[a, HIGHS], gr.at[15 + 2 * k])
     turn(4)
+    gather_targets(4)
     scores(4)
-
-    def pos_grads(t):
-        positive = jnp.sum(pos[:, TILES[t]], axis=0, keepdims=True)
-        return -jax.nn.sigmoid(-positive)
-
-    grads = [pos_grads(t) for t in range(4)]
-
-    def weights(d):
-        first = rows_of(d)
-        for t in range(4):
-            hit = one_hot(ids(tgt, t), first, J)
-            old = w[pl.ds(first, J), TILES[t]].astype(F32)
-            w[pl.ds(first, J), TILES[t]] = (old + jnp.where(hit, grads[t], 0.0)).astype(BF16)
+    from_negatives(4)
+
+    def finish(t):
+        q, target = qf[:, TILES[t]], tt[:, TILES[t]]
+        positive = jnp.sum(q * target, axis=0, keepdims=True)
+        pos_grad = -jax.nn.sigmoid(-positive)
+        tg[:, TILES[t]] = (pos_grad * q).astype(BF16)
+        g = pos_grad * target + gq[:, TILES[t]]
+        sg[:, TILES[t]] = back(g, os_[:, TILES[t]]).astype(BF16)
+        og[:, TILES[t]] = back(g, ss_[:, TILES[t]]).astype(BF16)
 
     def right_grad(d):
         zi = mod(me.z + d, 8)
-        part = dot_nt(qs[...], w[pl.ds(rows_of(d), J), :])
+        at = pl.ds(rows_of(d), J)
+        part = dot_nt(qs[...], w[at, :]) + dot_nt(tg[...], oht[at, :])
         rp[2 * zi] = part[:, :B]
         rp[2 * zi + 1] = part[:, B:]
 
     zto, xto, sign = (zp, zm), (xp, xm), (1, -1)
 
-    weights(4)
+    for t in range(4):
+        finish(t)
     right_grad(4)
     for k in (1, 0):
         rfar[k] = rp[me.left_at(4, k)].astype(BF16)
@@ -300,12 +326,6 @@
         for side in (0, 1):
             rows = pl.ds(0, LOW if side == 0 else HIGH)
             send(rfar.at[k, PART[side]], rb_half.at[side, k, rows], zs.at[side, 3, k], zr.at[side, 3, k], zto[side], r)
-    weights(3)
-    right_grad(3)
-    weights(-3)
-    right_grad(-3)
-    for d in (2, -2, 1, -1, 0):
-        weights(d)
 
     def right_step(d, k):
         for side, at in ((0, me.left_at(d, k)), (1, me.left_at(-d, k))):
@@ -324,24 +344,14 @@
             rstage[side, d - 1, k] = total.astype(BF16)
             send(rstage.at[side, d - 1, k], rb.at[side, d - 1, k], zs.at[side, d - 1, k], zr.at[side, d - 1, k], zto[side], r)
 
-    def query_grads(t):
-        g = dot(rcat(), w[:, TILES[t]])
-        sg[:, TILES[t]] = back(g, os_[:, TILES[t]]).astype(BF16)
-        og[:, TILES[t]] = back(g, ss_[:, TILES[t]]).astype(BF16)
-
-    query_grads(0)
-    right_step(3, 1)
-    right_step(3, 0)
-    for t in range(1, 4):
-        query_grads(t)
     part = dot_nt(ohr[...], og[...]).astype(BF16)
     for i in range(N):
         pp[i] = part[i * 16 : i * 16 + 16]
     for i in range(1, N):
         to = mod(r + i, N)
         send(pp.at[to], pbuf.at[i], ps.at[i], pr.at[i], l, to)
-    right_grad(2)
-    right_grad(-2)
+    right_grad(3)
+    right_grad(-3)
 
     order = ((2, 0), (2, 1), (1, 0), (-1, 0), (1, 1), (-1, 1), (0, 0), (0, 1))
 
@@ -359,10 +369,24 @@
         arrived(cbuf.at[n], cr.at[n])
         return lp[me.right_at(x, k)] + cbuf[n].astype(F32)
 
-    for n in range(6):
+    for n in range(4):
         left_grad(n)
-    right_step(2, 1)
-    right_step(2, 0)
+    right_step(3, 1)
+    right_step(3, 0)
+    left_grad(4)
+    left_grad(5)
+    right_grad(2)
+    right_grad(-2)
+    total = pp[r].astype(F32)
+    for i in range(1, N):
+        arrived(pbuf.at[i], pr.at[i])
+        total += pbuf[i].astype(F32)
+    for i in range(N):
+        prow[i] = total[i : i + 1]
+    for i in range(1, N):
+        to = mod(l + i, N)
+        send(prow.at[to], qbuf.at[i], qsm.at[i], qrm.at[i], to, r)
+
     for k in (1, 0):
         lstage[0, k] = chip_sum(k).astype(BF16)
         for side in (0, 1):
@@ -372,19 +396,9 @@
     left_grad(7)
     right_grad(1)
     right_grad(-1)
+    right_step(2, 1)
+    right_step(2, 0)
     right_grad(0)
-
-    total = pp[r].astype(F32)
-    for i in range(1, N):
-        arrived(pbuf.at[i], pr.at[i])
-        total += pbuf[i].astype(F32)
-    for i in range(N):
-        prow[i] = total[i : i + 1]
-    for i in range(1, N):
-        to = mod(l + i, N)
-        send(prow.at[to], qbuf.at[i], qsm.at[i], qrm.at[i], to, r)
-
-    right_step(1, 1)
     for k in (1, 0):
         for side in (0, 1):
             total = chip_sum(2 + 2 * k + side)
@@ -397,8 +411,6 @@
                 total = jnp.concatenate([total[:LOW], total[LOW:] + got], axis=0)
             lstage[1 + side, k] = total.astype(BF16)
             send(lstage.at[1 + side, k], lb.at[side, k], xs.at[side, 0, k], xr.at[side, 0, k], l, xto[side])
-    right_step(1, 0)
-
     total = prow[l]
     for i in range(1, N):
         arrived(qbuf.at[i], qrm.at[i])
@@ -407,6 +419,18 @@
     for i in range(1, N):
         to = mod(l + i, N)
         send(qrow.at[l], qrow.at[l], fs.at[i], fr.at[i], to, r)
+
+    right_step(1, 1)
+    right_step(1, 0)
+
+    for i in range(1, N):
+        arrived(qrow.at[mod(l - i, N)], fr.at[i])
+    total = jnp.concatenate([qrow[i] for i in range(N)], axis=0)
+    fown[...] = total.astype(BF16)
+    psum[r] = fown[...].astype(F32)
+    for i in range(1, N):
+        to = mod(r + i, N)
+        send(fown, fbuf.at[i], ps.at[N + i], pr.at[N + i], l, to)
 
     other = rp[me.left_at(0, 1)]
     for side in (0, 1):
@@ -426,14 +450,6 @@
         total += lb[side, 0].astype(F32)
     lsum[...] = total
 
-    for i in range(1, N):
-        arrived(qrow.at[mod(l - i, N)], fr.at[i])
-    fown[...] = jnp.concatenate([qrow[i] for i in range(N)], axis=0)
-    psum[r] = fown[...]
-    for i in range(1, N):
-        to = mod(r + i, N)
-        send(fown, fbuf.at[i], ps.at[N + i], pr.at[N + i], l, to)
-
     total = rp[l]
     for side in (0, 1):
         arrived(rb.at[side, 0, 0], zr.at[side, 0, 0])
@@ -446,7 +462,7 @@
     arrived(moved_state, ms.at[3])
     for i in range(1, N):
         arrived(fbuf.at[i], pr.at[N + i])
-        psum[mod(r - i, N)] = fbuf[i]
+        psum[mod(r - i, N)] = fbuf[i].astype(F32)
     for copy in sends:
         copy.wait_send()
 
@@ -461,7 +477,7 @@
             jax.ShapeDtypeStruct((W, B), F32),
             jax.ShapeDtypeStruct((W, B), F32),
             jax.ShapeDtypeStruct((N, 16, W), F32),
-            jax.ShapeDtypeStruct((B, W), F32),
+            jax.ShapeDtypeStruct((W, B), F32),
             jax.ShapeDtypeStruct((1, B), F32),
         ),
         in_specs=[vm] * 8,
@@ -482,10 +498,14 @@
             pltpu.VMEM((W, E), BF16),
             pltpu.VMEM((W, E), BF16),
             pltpu.VMEM((2, N * B, B), F32),
-            pltpu.VMEM((8, E), F32),
             pltpu.VMEM((N, W, B), F32),
             pltpu.VMEM((N, W, B), F32),
             pltpu.VMEM((N, 16, W), BF16),
+            pltpu.VMEM((N * B, E), BF16),
+            pltpu.VMEM((W, E), F32),
+            pltpu.VMEM((W, E), F32),
+            pltpu.VMEM((W, E), F32),
+            pltpu.VMEM((W, E), BF16),
             pltpu.VMEM((2, 2, LOW, B), BF16),
             pltpu.VMEM((2, 3, 2, W, B), BF16),
             pltpu.VMEM((2, 3, 2, W, B), BF16),
@@ -502,8 +522,8 @@
             pltpu.VMEM((N, 1, W), F32),
             pltpu.VMEM((N, 1, W), F32),
             pltpu.VMEM((N, 1, W), F32),
-            pltpu.VMEM((N, 16, W), F32),
-            pltpu.VMEM((16, W), F32),
+            pltpu.VMEM((N, 16, W), BF16),
+            pltpu.VMEM((16, W), BF16),
             dma((18,)), dma((18,)), dma((17,)), dma((17,)), dma((4,)),
             dma((2, 4, 2)), dma((2, 4, 2)),
             dma((8,)), dma((8,)),
@@ -520,19 +540,13 @@
 
 def update_kernel(left, left_state, lsum, moved, moved_state, rsum, rel, rel_state, psum, lo, lso, ro, rso, po, pso):
     for table, state, grad, out, state_out in (
-        (left, left_state, lsum, lo, lso),
-        (moved, moved_state, rsum, ro, rso),
+        (left, left_state, lsum[...], lo, lso),
+        (moved, moved_state, rsum[...], ro, rso),
+        (rel, rel_state, psum[...].reshape(256, W).T, po, pso),
     ):
-        g = grad[...]
-        new = state[...] + jnp.sum(g * g, axis=0, keepdims=True) * (1.0 / W)
+        new = state[...] + jnp.sum(grad * grad, axis=0, keepdims=True) * (1.0 / W)
         state_out[...] = new
-        out[...] = table[...] - (LEARN_RATE * g / jnp.sqrt(new)).T
-    g = psum[...].reshape(256, W)
-    mean = jnp.sum(g * g, axis=1, keepdims=True) * (1.0 / W)
-    state = jnp.broadcast_to(rel_state[...], (8, 256)).T[:, :1]
-    new = state + mean
-    po[...] = rel[...] - LEARN_RATE * g / jnp.sqrt(new)
-    pso[...] = jnp.broadcast_to(new, (256, 8)).T[:1]
+        out[...] = table[...] - LEARN_RATE * grad / jnp.sqrt(new)
 
 
 def update(*args):
@@ -540,11 +554,11 @@
     return pl.pallas_call(
         update_kernel,
         out_shape=(
-            jax.ShapeDtypeStruct((B, W), F32),
+            jax.ShapeDtypeStruct((W, B), F32),
             jax.ShapeDtypeStruct((1, B), F32),
-            jax.ShapeDtypeStruct((B, W), F32),
+            jax.ShapeDtypeStruct((W, B), F32),
             jax.ShapeDtypeStruct((1, B), F32),
-            jax.ShapeDtypeStruct((256, W), F32),
+            jax.ShapeDtypeStruct((W, 256), F32),
             jax.ShapeDtypeStruct((1, 256), F32),
         ),
         in_specs=[vm] * 9,
@@ -567,13 +581,13 @@
 ):
     row = lambda state: state.reshape(1, -1)
     lsum, rsum, psum, moved, moved_state = bucket(
-        left_table, right_table, row(right_state), relation_table, source_ids, relation_ids, target_ids, negative_ids
+        left_table.T, right_table.T, row(right_state), relation_table.T, source_ids, relation_ids, target_ids, negative_ids
     )
     left_new, left_state_new, right_new, right_state_new, relation_new, relation_state_new = update(
-        left_table, row(left_state), lsum, moved, moved_state, rsum, relation_table, row(relation_state), psum
+        left_table.T, row(left_state), lsum, moved, moved_state, rsum, relation_table.T, row(relation_state), psum
     )
     flat = lambda state: state.reshape(-1)
-    return (left_new, flat(left_state_new), right_new, flat(right_state_new), relation_new, flat(relation_state_new))
+    return (left_new.T, flat(left_state_new), right_new.T, flat(right_state_new), relation_new.T, flat(relation_state_new))
 
 
 def solution(mesh):

time: 88.8 us -> 75.7 us (0.85)
  local copies, waits for them, and re-layouts: 8.18 us -> 0 us
  Pallas kernels: 79.8 us -> 74.9 us
    unnamed x12 -> x0, local copies, waits for them, and re-layouts: 8.18 us -> none
    pallas_call x1, Pallas kernels: 76.9 us -> 72.2 us  [bucket(): pl.pallas_call(bucket_kernel, out_shape=(jax.ShapeDtypeStruct((W, B), F32...]
where the time goes in v3:
time: 75.7 us; the launch traced here: 75.6 us
  Pallas kernels  74.9 us (99%)
    pallas_call x1, Pallas kernels, bucket(): pl.pallas_call(bucket_kernel, out_shape=(jax.ShapeDtypeStruct((W, B), F32...  72.2 us
    pallas_call x1, Pallas kernels, update(): pl.pallas_call(update_kernel, out_shape=(jax.ShapeDtypeStruct((W, B), F32...  2.68 us

profile of v3, /device:TPU:1, one launch (start us, length us, event | category | flops | bytes accessed | tf_op | source)
XLA Modules:
  0.0 75.6 jit_solution(12494645856815798317)
XLA Ops:
  0.6 72.2 %bucket_round.1 = (f32[400,128]{1,0:T(8,128)}, f32[400,128]{1,0:T(8,128)}, f32[16,16,400]{2,1,0:T(8,128)}, f32[400,128]{1,0:T(8,128)}, f32[1,128]{1,0:T(1,128)}) custom-call(f32[400,128]{1,0:T(8,128)} %bitcast.14, f32[400,128]{1,0:T(8,128)} %bitcast.16, f32[1,128]{1,0:T(1,128)} %bitcast.19, f32[400,256]{1,0:T(8,128)} %bitcast.12, s32[1,1,1024]{2,1,0:T(1,128)} %src.1, ...), custom_call_target="tpu_custom_call" | custom-call | tf_op jit(solution)/shard_map/bucket_round/pallas_call | solution.py:474
  72.9 2.7 %update_tables.1 = (f32[400,128]{1,0:T(8,128)}, f32[1,128]{1,0:T(1,128)}, f32[400,128]{1,0:T(8,128)}, f32[1,128]{1,0:T(1,128)}, f32[400,256]{1,0:T(8,128)}, /*index=5*/f32[1,256]{1,0:T(1,128)}) custom-call(f32[400,128]{1,0:T(8,128)} %bitcast.15, f32[1,128]{1,0:T(1,128)} %bitcast.18, f32[400,128]{1,0:T(8,128)} %get-tuple-element.17.lsum, ...), custom_call_target="tpu_custom_call" | custom-call | tf_op jit(solution)/shard_map/update_tables/pallas_call | solution.py:554

commit v4 on v3

--- a/solution.py
+++ b/solution.py
@@ -108,7 +108,7 @@
     def greet(a, b):
         pl.semaphore_signal(barrier, inc=1, device_id=(a, b), device_id_type=MESH)
 
-    peers = [(a, b) for a in (l_other, zp, zm) for b in (ahead, behind)]
+    peers = [(l_other, ahead), (l_other, behind)]
     peers += [(l, mod(r + i, N)) for i in range(1, N)] + [(mod(l + i, N), r) for i in range(1, N)]
     for a, b in peers:
         greet(a, b)
@@ -129,9 +129,13 @@
     rel[...] = relation[...].astype(BF16)
     ids = lambda ref, t: ref[0, :, TILES[t]]
 
-    def counts(c, j):
-        hit = jnp.where(one_hot(neg[0, 0, c : c + 1, :], j * J, J), NEG_WEIGHT, 0.0)
-        mult[c, pl.ds(j * J, J), :] = jnp.broadcast_to(jnp.sum(hit, axis=1, keepdims=True), (J, B))
+    def counts(c):
+        named = neg[0, 0, c : c + 1, :]
+        low_hot = ones(one_hot(lax.bitwise_and(named, B - 1), 0, B))
+        block_hot = ones(one_hot(lax.shift_right_logical(named, 7), 0, B))
+        count = dot_nt(low_hot, block_hot) * NEG_WEIGHT
+        for i in range(N):
+            mult[c, pl.ds(i * B, B), :] = jnp.broadcast_to(count[:, i : i + 1], (B, B))
 
     def source_hot(j):
         ohs[pl.ds(j * J, J), :] = ones(one_hot(src[0], j * J, J))
@@ -140,10 +144,8 @@
     ohr[...] = ones(one_hot(rid[0], 0, 256))
     pl.semaphore_wait(barrier, len(peers))
 
+    send(rt, rg.at[l], gs.at[0], gr.at[0], l, ahead)
     send(rt, rg.at[l], gs.at[1], gr.at[1], l_other, ahead)
-    send(rt, rg.at[l], gs.at[2], gr.at[2], zp, ahead)
-    send(rt, rg.at[l], gs.at[3], gr.at[3], zm, ahead)
-    send(rt, rg.at[l], gs.at[0], gr.at[0], l, ahead)
     send(lt, lg.at[r], ls.at[0], lr.at[0], l, yo)
     send(lt, lg.at[r], ls.at[1], lr.at[1], l, xp)
     send(lt, lg.at[r], ls.at[2], lr.at[2], l, xm)
@@ -177,38 +179,6 @@
         arrived(lg.at[a, HIGHS], lr.at[i + 1])
         send(lg.at[a], lg.at[a], ls.at[15 + k], lr.at[15 + k], l, co)
 
-    for j in range(4):
-        counts(0, j)
-    arrived(lg.at[yo], lr.at[0])
-    send(lg.at[yo], lg.at[yo], ls.at[4], lr.at[4], l, xp)
-    send(lg.at[yo], lg.at[yo], ls.at[5], lr.at[5], l, xm)
-    send(lg.at[yo], lg.at[yo], ls.at[6], lr.at[6], l, co)
-    across(0)
-    for j in range(4, 6):
-        counts(0, j)
-    arrived(rg.at[l_other], gr.at[1])
-    send(rg.at[l_other], rg.at[l_other], gs.at[4], gr.at[4], zp, r)
-    send(rg.at[l_other], rg.at[l_other], gs.at[5], gr.at[5], zm, r)
-    counts(0, 6)
-    counts(0, 7)
-    ring(1, 0)
-    counts(1, 0)
-    across(1)
-    for j in range(1, 5):
-        counts(1, j)
-    ring(1, 1)
-    for j in range(5, 8):
-        counts(1, j)
-    far(0)
-    for j in range(3):
-        source_hot(j)
-    ring(2, 0)
-    far(1)
-    for j in range(3, 8):
-        source_hot(j)
-    for t in range(4):
-        os_[:, TILES[t]] = dot(rel[...], ohr[:, TILES[t]])
-
     lcat = lambda: jnp.concatenate([lg[i] for i in range(N)], axis=1)
 
     def slots_of(*ds):
@@ -256,9 +226,38 @@
             m = jnp.concatenate([m, m], axis=1)
             w[pl.ds(first, J), TILES[t]] = (jax.nn.sigmoid(score) * m).astype(BF16)
 
+    counts(0)
+    counts(1)
     arrived(rg.at[l], gr.at[0])
+    send(rg.at[l], rg.at[l], gs.at[2], gr.at[2], zp, r)
+    send(rg.at[l], rg.at[l], gs.at[3], gr.at[3], zm, r)
+    arrived(lg.at[yo], lr.at[0])
+    send(lg.at[yo], lg.at[yo], ls.at[4], lr.at[4], l, xp)
+    send(lg.at[yo], lg.at[yo], ls.at[5], lr.at[5], l, xm)
+    send(lg.at[yo], lg.at[yo], ls.at[6], lr.at[6], l, co)
+    across(0)
+    source_hot(0)
+    source_hot(1)
+    arrived(rg.at[l_other], gr.at[1])
+    send(rg.at[l_other], rg.at[l_other], gs.at[4], gr.at[4], zp, r)
+    send(rg.at[l_other], rg.at[l_other], gs.at[5], gr.at[5], zm, r)
+    for j in range(2, 6):
+        source_hot(j)
+    ring(1, 0)
+    across(1)
+    source_hot(6)
+    source_hot(7)
     turn(0)
     gather_targets(0)
+    far(0)
+    ring(1, 1)
+    for t in range(4):
+        os_[:, TILES[t]] = dot(rel[...], ohr[:, TILES[t]])
+    far(1)
+    turn(1)
+    turn(-1)
+    ring(2, 0)
+    gather_targets(1, -1)
     for x, k, i in ((0, 0, 3), (0, 1, 6), (-1, 0, 9), (1, 0, 10), (-1, 1, 13), (1, 1, 14), (2, 0, 15), (2, 1, 16)):
         arrived(lg.at[me.right_at(x, k, 1)], lr.at[i])
     queries(0)
@@ -270,18 +269,15 @@
     queries(3)
     scores(0)
     from_negatives(0)
-    turn(1)
-    turn(-1)
+    scores(1)
     ring(3, 0)
-    gather_targets(1, -1)
-    scores(1)
     scores(-1)
     from_negatives(1, -1)
-    ring(3, 1)
     turn(2)
     turn(-2)
     gather_targets(2, -2)
     scores(2)
+    ring(3, 1)
     scores(-2)
     from_negatives(2, -2)
     turn(3)

time: 75.7 us -> 71.3 us (0.942)
  Pallas kernels: 74.9 us -> 70.5 us
    pallas_call x1, Pallas kernels: 72.2 us -> 67.9 us  [bucket(): pl.pallas_call(bucket_kernel, out_shape=(jax.ShapeDtypeStruct((W, B), F32...]
where the time goes in v4:
time: 71.3 us; the launch traced here: 71.2 us
  Pallas kernels  70.5 us (99%)
    pallas_call x1, Pallas kernels, bucket(): pl.pallas_call(bucket_kernel, out_shape=(jax.ShapeDtypeStruct((W, B), F32...  67.9 us
    pallas_call x1, Pallas kernels, update(): pl.pallas_call(update_kernel, out_shape=(jax.ShapeDtypeStruct((W, B), F32...  2.68 us

profile of v4, /device:TPU:1, one launch (start us, length us, event | category | flops | bytes accessed | tf_op | source)
XLA Modules:
  0.0 71.2 jit_solution(12583348359856238409)
XLA Ops:
  0.6 67.9 %bucket_round.1 = (f32[400,128]{1,0:T(8,128)}, f32[400,128]{1,0:T(8,128)}, f32[16,16,400]{2,1,0:T(8,128)}, f32[400,128]{1,0:T(8,128)}, f32[1,128]{1,0:T(1,128)}) custom-call(f32[400,128]{1,0:T(8,128)} %bitcast.14, f32[400,128]{1,0:T(8,128)} %bitcast.16, f32[1,128]{1,0:T(1,128)} %bitcast.19, f32[400,256]{1,0:T(8,128)} %bitcast.12, s32[1,1,1024]{2,1,0:T(1,128)} %src.1, ...), custom_call_target="tpu_custom_call" | custom-call | tf_op jit(solution)/shard_map/bucket_round/pallas_call | solution.py:470
  68.5 2.7 %update_tables.1 = (f32[400,128]{1,0:T(8,128)}, f32[1,128]{1,0:T(1,128)}, f32[400,128]{1,0:T(8,128)}, f32[1,128]{1,0:T(1,128)}, f32[400,256]{1,0:T(8,128)}, /*index=5*/f32[1,256]{1,0:T(1,128)}) custom-call(f32[400,128]{1,0:T(8,128)} %bitcast.15, f32[1,128]{1,0:T(1,128)} %bitcast.18, f32[400,128]{1,0:T(8,128)} %get-tuple-element.17.lsum, ...), custom_call_target="tpu_custom_call" | custom-call | tf_op jit(solution)/shard_map/update_tables/pallas_call | solution.py:550

commit v5 on v4

--- a/solution.py
+++ b/solution.py
@@ -293,14 +293,16 @@
     turn(4)
     gather_targets(4)
     scores(4)
-    from_negatives(4)
-
-    def finish(t):
-        q, target = qf[:, TILES[t]], tt[:, TILES[t]]
-        positive = jnp.sum(q * target, axis=0, keepdims=True)
+
+    def positive_grad(t):
+        q = qf[:, TILES[t]]
+        positive = jnp.sum(q * tt[:, TILES[t]], axis=0, keepdims=True)
         pos_grad = -jax.nn.sigmoid(-positive)
         tg[:, TILES[t]] = (pos_grad * q).astype(BF16)
-        g = pos_grad * target + gq[:, TILES[t]]
+        return pos_grad
+
+    def query_grad(t):
+        g = pos_grads[t] * tt[:, TILES[t]] + gq[:, TILES[t]]
         sg[:, TILES[t]] = back(g, os_[:, TILES[t]]).astype(BF16)
         og[:, TILES[t]] = back(g, ss_[:, TILES[t]]).astype(BF16)
 
@@ -313,8 +315,7 @@
 
     zto, xto, sign = (zp, zm), (xp, xm), (1, -1)
 
-    for t in range(4):
-        finish(t)
+    pos_grads = [positive_grad(t) for t in range(4)]
     right_grad(4)
     for k in (1, 0):
         rfar[k] = rp[me.left_at(4, k)].astype(BF16)
@@ -340,6 +341,9 @@
             rstage[side, d - 1, k] = total.astype(BF16)
             send(rstage.at[side, d - 1, k], rb.at[side, d - 1, k], zs.at[side, d - 1, k], zr.at[side, d - 1, k], zto[side], r)
 
+    from_negatives(4)
+    for t in range(4):
+        query_grad(t)
     part = dot_nt(ohr[...], og[...]).astype(BF16)
     for i in range(N):
         pp[i] = part[i * 16 : i * 16 + 16]
@@ -423,7 +427,7 @@
         arrived(qrow.at[mod(l - i, N)], fr.at[i])
     total = jnp.concatenate([qrow[i] for i in range(N)], axis=0)
     fown[...] = total.astype(BF16)
-    psum[r] = fown[...].astype(F32)
+    psum[r] = fown[...]
     for i in range(1, N):
         to = mod(r + i, N)
         send(fown, fbuf.at[i], ps.at[N + i], pr.at[N + i], l, to)
@@ -458,7 +462,7 @@
     arrived(moved_state, ms.at[3])
     for i in range(1, N):
         arrived(fbuf.at[i], pr.at[N + i])
-        psum[mod(r - i, N)] = fbuf[i].astype(F32)
+        psum[mod(r - i, N)] = fbuf[i]
     for copy in sends:
         copy.wait_send()
 
@@ -472,7 +476,7 @@
         out_shape=(
             jax.ShapeDtypeStruct((W, B), F32),
             jax.ShapeDtypeStruct((W, B), F32),
-            jax.ShapeDtypeStruct((N, 16, W), F32),
+            jax.ShapeDtypeStruct((N, 16, W), BF16),
             jax.ShapeDtypeStruct((W, B), F32),
             jax.ShapeDtypeStruct((1, B), F32),
         ),
@@ -538,7 +542,7 @@
     for table, state, grad, out, state_out in (
         (left, left_state, lsum[...], lo, lso),
         (moved, moved_state, rsum[...], ro, rso),
-        (rel, rel_state, psum[...].reshape(256, W).T, po, pso),
+        (rel, rel_state, psum[...].reshape(256, W).astype(F32).T, po, pso),
     ):
         new = state[...] + jnp.sum(grad * grad, axis=0, keepdims=True) * (1.0 / W)
         state_out[...] = new

time: 71.3 us -> 71.4 us (level)
  no operation moved by 1% of the time
where the time goes in v5:
time: 71.4 us; the launch traced here: 71 us
  Pallas kernels  70.4 us (99%)
    pallas_call x1, Pallas kernels, bucket(): pl.pallas_call(bucket_kernel, out_shape=(jax.ShapeDtypeStruct((W, B), F32...  67.7 us
    pallas_call x1, Pallas kernels, update(): pl.pallas_call(update_kernel, out_shape=(jax.ShapeDtypeStruct((W, B), F32...  2.63 us

profile of v5, /device:TPU:1, one launch (start us, length us, event | category | flops | bytes accessed | tf_op | source)
XLA Modules:
  0.0 71.0 jit_solution(5663248275956715396)
XLA Ops:
  0.6 67.7 %bucket_round.1 = (f32[400,128]{1,0:T(8,128)}, f32[400,128]{1,0:T(8,128)}, bf16[16,16,400]{2,1,0:T(8,128)(2,1)}, f32[400,128]{1,0:T(8,128)}, f32[1,128]{1,0:T(1,128)}) custom-call(f32[400,128]{1,0:T(8,128)} %bitcast.14, f32[400,128]{1,0:T(8,128)} %bitcast.16, f32[1,128]{1,0:T(1,128)} %bitcast.19, f32[400,256]{1,0:T(8,128)} %bitcast.12, s32[1,1,1024]{2,1,0:T(1,128)} %src.1, ...), custom_call_target="tpu_custom_call" | custom-call | tf_op jit(solution)/shard_map/bucket_round/pallas_call | solution.py:474
  68.4 2.6 %update_tables.1 = (f32[400,128]{1,0:T(8,128)}, f32[1,128]{1,0:T(1,128)}, f32[400,128]{1,0:T(8,128)}, f32[1,128]{1,0:T(1,128)}, f32[400,256]{1,0:T(8,128)}, /*index=5*/f32[1,256]{1,0:T(1,128)}) custom-call(f32[400,128]{1,0:T(8,128)} %bitcast.15, f32[1,128]{1,0:T(1,128)} %bitcast.18, f32[400,128]{1,0:T(8,128)} %get-tuple-element.17.lsum, ...), custom_call_target="tpu_custom_call" | custom-call | tf_op jit(solution)/shard_map/update_tables/pallas_call | solution.py:554
